TPU v7x, 256 devices: a whole 4x4x8 slice. The times are simulated.
256 devices in a mesh: strike: 64 (over z, y_hi, x), dip: 4 (over y_lo, core).
Axes of the slice: x: 4, y: 4 (y_hi: 2, y_lo: 2; y = y_hi * 2 + y_lo), z: 8, core: 2. Of those that a mesh axis runs over, the one named last changes fastest.
Arguments:
- coarse_field: bfloat16 [256, 16, 128], P('strike', 'dip'), may hold values from -6 to 6
- up_weight: bfloat16 [8, 8, 8, 32, 32], replicated, may hold values from -0.375 to 0.375
- first_weight: bfloat16 [3, 3, 3, 32, 32], replicated, may hold values from -0.21875 to 0.21875
- second_weight: bfloat16 [3, 3, 3, 32, 32], replicated, may hold values from -0.21875 to 0.21875
Outputs:
- refined: bfloat16 [1024, 64, 512], P('strike', 'dip')
All inputs are finite; a program needn't handle non-finite values.
Results may differ from a plain program's by a relative error of at most 0.012.
Values may be sent and summed in bfloat16 or wider, within the bound.
A program may use at most 192 MiB of HBM per device.

v0:
```python
import jax
import jax.numpy as jnp
import numpy as np
from jax import lax
from jax.experimental import pallas as pl
from jax.experimental.pallas import tpu as pltpu
from jax.sharding import PartitionSpec as P

HIGHEST = lax.Precision.HIGHEST


def extended_2(cells, sides, width):
    for axis, dim in sides:
        count = lax.axis_size(axis)
        ends = count - 1
        head = lax.slice_in_dim(cells, 0, width, axis=dim)
        tail = lax.slice_in_dim(cells, cells.shape[dim] - width, cells.shape[dim], axis=dim)
        cells = jnp.concatenate(
            [
                lax.ppermute(tail, axis, [(i, (i + 1) % count) for i in range(ends)]),
                cells,
                lax.ppermute(head, axis, [((i + 1) % count, i) for i in range(ends)]),
            ],
            axis=dim,
        )
    return cells


def up_tables(up_weight, coarse_depth):
    channels = up_weight.shape[3]
    fine_depth = 4 * coarse_depth
    zero = jnp.zeros((), up_weight.dtype)
    taps = up_weight.reshape(2, 4, 2, 4, 8, channels, channels).transpose(0, 2, 1, 3, 5, 4, 6)
    taps = taps.reshape(2, 2, 4, 4, channels, 8 * channels)
    keep = [(0, 0, 0)] * 5
    return jnp.concatenate(
        [
            lax.pad(
                taps,
                zero,
                keep + [(channels * (4 * c - 2), channels * (fine_depth - 4 * c - 6), 0)],
            )
            for c in range(coarse_depth)
        ],
        axis=4,
    )


def spread(coarse_block, up_mats):
    size_one, size_two, depth_lanes = coarse_block.shape
    lane_width = up_mats.shape[5]
    flat_rows = coarse_block.reshape(size_one * size_two, depth_lanes)
    stacked = up_mats.reshape(64, depth_lanes, lane_width)
    product = jnp.einsum(
        "bpk,bkn->bpn",
        jnp.broadcast_to(flat_rows, (64,) + flat_rows.shape),
        stacked,
        preferred_element_type=jnp.float32,
    )
    product = product.reshape(2, 2, 4, 4, size_one, size_two, lane_width)
    summed = jnp.zeros((4, 4, size_one + 1, size_two + 1, lane_width), jnp.float32)
    for high_one in (0, 1):
        for high_two in (0, 1):
            summed = summed + jnp.pad(
                product[high_one, high_two],
                ((0, 0), (0, 0), (high_one, 1 - high_one), (high_two, 1 - high_two), (0, 0)),
            )
    summed = summed.transpose(2, 0, 3, 1, 4)
    return summed.reshape(4 * size_one + 4, 4 * size_two + 4, lane_width)


def full_band(weight):
    channels = weight.shape[3]
    depth = 16
    zero = jnp.zeros((), weight.dtype)
    taps = weight[:, :, ::-1].transpose(0, 1, 3, 2, 4).reshape(3, 3, channels, 3 * channels)
    keep = [(0, 0, 0)] * 3
    band = jnp.concatenate(
        [
            lax.pad(taps, zero, keep + [(channels * (c - 1), channels * (depth - c - 2), 0)])
            for c in range(depth)
        ],
        axis=2,
    )
    return band.reshape(9, depth * channels, depth * channels)


def inside(axis, count, own, halo):
    place = lax.axis_index(axis)
    local = jnp.arange(count) - halo
    return ((local >= 0) | (place > 0)) & ((local < own) | (place < lax.axis_size(axis) - 1))


def masked_silu(values, own_rows, own_cols, halo):
    rows = inside("strike", values.shape[0], own_rows, halo)
    cols = inside("dip", values.shape[1], own_cols, halo)
    keep = rows[:, None, None] & cols[None, :, None]
    return jnp.where(keep, jax.nn.silu(values), 0.0).astype(jnp.bfloat16)


def shifted(values, width):
    rows = values.shape[0]
    return (
        pltpu.roll(values, 1, 0).astype(jnp.bfloat16),
        values.astype(jnp.bfloat16),
        pltpu.roll(values, rows - 1, 0).astype(jnp.bfloat16),
    )


def conv_rows(parts, band_ref, width, count):
    total = None
    for one in range(3):
        for two in range(3):
            window = parts[two][one * width : one * width + count]
            term = jnp.dot(window, band_ref[one * 3 + two], preferred_element_type=jnp.float32)
            total = term if total is None else total + term
    return total


def convs_kernel(width, rows_out, cols_out, base_ref, keep_ref, first_ref, second_ref, out_ref):
    base = base_ref[...].astype(jnp.float32)
    hidden_count = (rows_out + 2) * width
    first = conv_rows(shifted(base, width), first_ref, width, hidden_count)
    hidden = jnp.where(keep_ref[...] > 0, first / (1.0 + jnp.exp(-first)), 0.0)
    out_count = rows_out * width
    second = conv_rows(shifted(hidden, width), second_ref, width, out_count)
    summed = base[2 * width : 2 * width + out_count] + second
    summed = pltpu.roll(summed, out_count - 2, 0).reshape(rows_out, width, summed.shape[1])
    out_ref[...] = summed[:, :cols_out].astype(out_ref.dtype)


def body(coarse_field, up_weight, first_weight, second_weight):
    channels = up_weight.shape[3]
    coarse_depth = coarse_field.shape[2] // channels
    up_mats = up_tables(up_weight, coarse_depth)
    own_rows = 4 * coarse_field.shape[0]
    own_cols = 4 * coarse_field.shape[1]
    lanes = 4 * coarse_depth * channels
    width = 32
    coarse_ext = extended_2(coarse_field, (("strike", 0), ("dip", 1)), 1)
    extended = spread(coarse_ext, up_mats)[4 : own_rows + 8, 4 : own_cols + 8]
    base = masked_silu(extended, own_rows, own_cols, 2)
    base = jnp.pad(base, ((0, 0), (0, width - own_cols - 4), (0, 0))).reshape(-1, lanes)
    rows_keep = inside("strike", own_rows + 4, own_rows, 2)[1 : own_rows + 3]
    cols_keep = inside("dip", own_cols + 4, own_cols, 2) & (jnp.arange(own_cols + 4) >= 1)
    cols_keep = jnp.pad(cols_keep & (jnp.arange(own_cols + 4) < own_cols + 3), (0, width - own_cols - 4))
    keep = (rows_keep[:, None] & cols_keep[None, :]).astype(jnp.float32).reshape(-1, 1)
    vmem = pl.BlockSpec(memory_space=pltpu.VMEM)
    return pl.pallas_call(
        lambda *refs: convs_kernel(width, own_rows, own_cols, *refs),
        out_shape=jax.ShapeDtypeStruct((own_rows, own_cols, lanes), jnp.bfloat16),
        in_specs=[vmem] * 4,
        out_specs=vmem,
    )(base, keep, full_band(first_weight), full_band(second_weight))


def solution(mesh):
    return jax.shard_map(
        body,
        mesh=mesh,
        in_specs=(P("strike", "dip", None), P(), P(), P()),
        out_specs=P("strike", "dip", None),
        check_vma=False,
    )
```

profile of v0, /device:TPU:119, one launch (start us, length us, event | category | flops | bytes accessed | tf_op | source)
XLA Modules:
  0.0 91.7 jit_solution(13219194316218274535)
XLA Ops:
  0.7 2.4 %collective-permute-start.1 = (bf16[1,4,128]{2,1,0:T(4,128)(2,1)S(1)}, bf16[1,4,128]{2,1,0:T(4,128)(2,1)S(1)}, u32[]{:S(2)}, u32[]{:S(2)}) collective-permute-start(bf16[1,4,128]{2,1,0:T(4,128)(2,1)S(1)} %get-tuple-element.15), channel_id=1, source_target_pairs={{4,0},{8,4},{12,8},{16,12},{20,16},{24,20},{28,24},{32,28},{36,32}... | collective-permute-start | bytes 3080 | tf_op jit(solution)/shard_map/ppermute | solution.py:22
  3.2 8.5 %collective-permute-start = (bf16[1,4,128]{2,1,0:T(4,128)(2,1)S(1)}, bf16[1,4,128]{2,1,0:T(4,128)(2,1)S(1)}, u32[]{:S(2)}, u32[]{:S(2)}) collective-permute-start(bf16[1,4,128]{2,1,0:T(4,128)(2,1)S(1)} %get-tuple-element.16), channel_id=1, source_target_pairs={{0,4},{4,8},{8,12},{12,16},{16,20},{20,24},{24,28},{28,32},{32,36}... | collective-permute-start | bytes 3080 | tf_op jit(solution)/shard_map/ppermute | solution.py:20
  11.9 1.0 %reverse_bitcast_fusion.1 = bf16[3,3,32,3,32]{4,2,3,1,0:T(8,128)(2,1)S(1)} fusion(bf16[3,3,3,32,32]{4,3,2,1,0:T(8,128)(2,1)} %param.6), kind=kLoop, calls=%fused_computation.58 | loop fusion | bytes 110592 | tf_op jit(solution)/shard_map/transpose | solution.py:76
  13.2 1.0 %reverse_bitcast_fusion = bf16[3,3,32,3,32]{4,2,3,1,0:T(8,128)(2,1)S(1)} fusion(bf16[3,3,3,32,32]{4,3,2,1,0:T(8,128)(2,1)} %param.7), kind=kLoop, calls=%fused_computation.57 | loop fusion | bytes 110592 | tf_op jit(solution)/shard_map/transpose | solution.py:76
  14.5 8.3 %copy.15 = bf16[2,2,4,4,32,8,32]{6,5,4,3,2,1,0:T(8,128)(2,1)} copy(bf16[2,2,4,4,32,8,32]{6,4,5,3,1,2,0:T(8,128)(2,1)} %bitcast.34) | data formatting | bytes 2097152 | tf_op jit(solution)/shard_map/transpose | solution.py:33
  22.8 5.3 %reshape.115 = bf16[2,2,4,4,32,256]{5,4,3,2,1,0:T(8,128)(2,1)S(1)} reshape(bf16[2,2,4,4,32,8,32]{6,5,4,3,2,1,0:T(8,128)(2,1)} %copy.15) | data formatting | bytes 2097152 | tf_op jit(solution)/shard_map/reshape | solution.py:34
  28.1 1.1 %pad_slice_fusion.1 = (bf16[2,2,4,4,32,512]{5,4,3,2,1,0:T(8,128)(2,1)S(1)}, bf16[2,2,4,4,32,512]{5,4,3,2,1,0:T(8,128)(2,1)S(1)}) fusion(bf16[2,2,4,4,32,256]{5,4,3,2,1,0:T(8,128)(2,1)S(1)} %reshape.115), kind=kLoop, calls=%fused_computation.12 | loop fusion | bytes 5242880 | tf_op jit(solution)/shard_map/pad | solution.py:38
  30.7 2.2 %copy-done = bf16[3,3,512,512]{3,2,1,0:T(8,128)(2,1)} copy-done((bf16[3,3,512,512]{3,2,1,0:T(8,128)(2,1)}, bf16[3,3,512,512]{3,2,1,0:T(8,128)(2,1)S(1)}, u32[]{:S(2)}) %copy-start) | copy-done | bytes 4718616
  32.9 0.8 fusion.9
  34.5 0.9 pad_dynamic-update-slice_fusion.26
  35.4 0.9 pad_dynamic-update-slice_fusion.25
  36.3 0.9 pad_dynamic-update-slice_fusion.24
  38.0 0.8 pad_dynamic-update-slice_fusion.22
  38.8 0.8 pad_dynamic-update-slice_fusion.21
  39.6 0.8 pad_dynamic-update-slice_fusion.20
  41.2 0.9 pad_dynamic-update-slice_fusion.18
  42.1 0.9 pad_dynamic-update-slice_fusion.17
  43.0 0.8 pad_dynamic-update-slice_fusion.16
  44.6 4.4 %fusion.5 = bf16[2,2,4,4,128,512]{5,4,3,2,1,0:T(8,128)(2,1)} fusion(bf16[2,2,4,4,32,256]{5,4,3,2,1,0:T(8,128)(2,1)S(1)} %reshape.115, bf16[2,2,4,4,32,512]{5,4,3,2,1,0:T(8,128)(2,1)S(1)} %get-tuple-element.12, bf16[2,2,4,4,32,512]{5,4,3,2,1,0:T(8,128)(2,1)S(1)} %get-tuple-element.11), kind=kLoop, calls=%fused_computation.9 | loop fusion | flops 67108864 | bytes 13631488 | tf_op jit(solution)/shard_map/concatenate | solution.py:36
  49.1 0.8 pad_dynamic-update-slice_fusion.14
  49.9 4.0 %collective-permute-start.2 = (bf16[6,1,128]{2,1,0:T(2,128)(2,1)S(1)}, bf16[6,1,128]{2,1,0:T(2,128)(2,1)S(1)}, u32[]{:S(2)}, u32[]{:S(2)}) collective-permute-start(bf16[6,1,128]{2,1,0:T(2,128)(2,1)S(1)} %get-tuple-element.13), channel_id=1, source_target_pairs={{0,1},{1,2},{2,3},{4,5},{5,6},{6,7},{8,9},{9,10},{10,11},{12,13},{... | collective-permute-start | bytes 4616 | tf_op jit(solution)/shard_map/ppermute | solution.py:20
  54.0 2.1 %collective-permute-start.3 = (bf16[6,1,128]{2,1,0:T(2,128)(2,1)S(1)}, bf16[6,1,128]{2,1,0:T(2,128)(2,1)S(1)}, u32[]{:S(2)}, u32[]{:S(2)}) collective-permute-start(bf16[6,1,128]{2,1,0:T(2,128)(2,1)S(1)} %get-tuple-element.14), channel_id=1, source_target_pairs={{1,0},{2,1},{3,2},{5,4},{6,5},{7,6},{9,8},{10,9},{11,10},{13,12},{... | collective-permute-start | bytes 4616 | tf_op jit(solution)/shard_map/ppermute | solution.py:22
  56.1 0.8 fusion.10
  56.9 1.0 %reshape.125.refs_1_ = f32[576,1]{1,0:T(8,128)} reshape(f32[18,32]{1,0:T(8,128)S(1)} %and_convert_fusion) | data formatting | bytes 4608 | tf_op jit(solution)/shard_map/convert_element_type | solution.py:147
  57.9 1.0 %collective-permute-done.3 = bf16[6,1,128]{2,1,0:T(2,128)(2,1)S(1)} collective-permute-done((bf16[6,1,128]{2,1,0:T(2,128)(2,1)S(1)}, bf16[6,1,128]{2,1,0:T(2,128)(2,1)S(1)}, u32[]{:S(2)}, u32[]{:S(2)}) %collective-permute-start.3) | collective-permute-done | bytes 1568 | tf_op jit(solution)/shard_map/ppermute | solution.py:22
  58.9 4.6 %fusion.7 = f32[64,36,512]{2,1,0:T(8,128)S(1)} fusion(bf16[64,128,512]{2,1,0:T(8,128)(2,1)} %bitcast.32, bf16[36,128]{1,0:T(8,128)(2,1)S(1)} %reshape.113), kind=kOutput, calls=%fused_computation.23 | convolution fusion | flops 301989888 | bytes 13116416 | tf_op jit(solution)/shard_map/bpk,bkn->bpn/dot_general | solution.py:54
  63.6 5.0 %copy.16 = f32[64,36,512]{2,0,1:T(8,128)} copy(f32[64,36,512]{2,1,0:T(8,128)S(1)} %fusion.7) | data formatting | bytes 9437184 | tf_op jit(solution)/shard_map/bpk,bkn->bpn/dot_general | solution.py:54
  68.5 6.3 %reshape.117 = f32[2,2,4,4,6,6,512]{6,3,2,1,0,5,4:T(4,128)} reshape(f32[64,36,512]{2,0,1:T(8,128)} %copy.16) | data formatting | bytes 9437184 | tf_op jit(solution)/shard_map/reshape | solution.py:60
  74.8 3.3 %slice_bitcast_fusion.3 = (f32[4,4,6,6,512]{4,1,0,3,2:T(4,128)S(1)}, f32[4,4,6,6,512]{4,1,0,3,2:T(4,128)S(1)}, f32[4,4,6,6,512]{4,1,0,3,2:T(4,128)S(1)}, f32[4,4,6,6,512]{4,1,0,3,2:T(4,128)S(1)}) fusion(f32[2,2,4,4,6,6,512]{6,3,2,1,0,5,4:T(4,128)} %reshape.117), kind=kLoop, calls=%fused_computation.17 | loop fusion | bytes 9437184 | tf_op jit(solution)/shard_map/squeeze | solution.py:65
  78.1 0.9 %add_bitcast_fusion = f32[7,4,7,4,512]{4,3,1,2,0:T(4,128)S(1)} fusion(f32[4,4,6,6,512]{4,1,0,3,2:T(4,128)S(1)} %get-tuple-element.9, f32[4,4,6,6,512]{4,1,0,3,2:T(4,128)S(1)} %get-tuple-element.10, f32[4,4,6,6,512]{4,1,0,3,2:T(4,128)S(1)} %get-tuple-element.8, f32[4,4,6,6,512]{4,1,0,3,2:T(4,128)S(1)} %get-tuple-element.7), kind=kLoop, calls=%fused_computation.13 | loop fusion | flops 1204224 | bytes 6324224 | tf_op jit(solution)/shard_map/transpose | solution.py:68
  80.3 0.9 pad.160
  81.2 10.6 %shard_map.46 = bf16[16,16,512]{2,1,0:T(8,128)(2,1)} custom-call(bf16[640,512]{1,0:T(8,128)(2,1)} %bitcast.35, f32[576,1]{1,0:T(8,128)} %reshape.125.refs_1_, bf16[9,512,512]{2,1,0:T(8,128)(2,1)} %bitcast.10.refs_2_, bf16[9,512,512]{2,1,0:T(8,128)(2,1)} %bitcast.33), custom_call_target="tpu_custom_call" | custom-call | tf_op jit(solution)/shard_map/pallas_call | solution.py:149
  (45 shorter events, 7.3 us)
Async XLA Ops:
  0.7 49.2 %collective-permute-start.1 = (bf16[1,4,128]{2,1,0:T(4,128)(2,1)S(1)}, bf16[1,4,128]{2,1,0:T(4,128)(2,1)S(1)}, u32[]{:S(2)}, u32[]{:S(2)}) collective-permute-start(bf16[1,4,128]{2,1,0:T(4,128)(2,1)S(1)} %get-tuple-element.15), channel_id=1, source_target_pairs={{4,0},{8,4},{12,8},{16,12},{20,16},{24,20},{28,24},{32,28},{36,32}... | collective-permute-start | bytes 3080 | tf_op jit(solution)/shard_map/ppermute | solution.py:22
  3.2 46.7 %collective-permute-start = (bf16[1,4,128]{2,1,0:T(4,128)(2,1)S(1)}, bf16[1,4,128]{2,1,0:T(4,128)(2,1)S(1)}, u32[]{:S(2)}, u32[]{:S(2)}) collective-permute-start(bf16[1,4,128]{2,1,0:T(4,128)(2,1)S(1)} %get-tuple-element.16), channel_id=1, source_target_pairs={{0,4},{4,8},{8,12},{12,16},{16,20},{20,24},{24,28},{28,32},{32,36}... | collective-permute-start | bytes 3080 | tf_op jit(solution)/shard_map/ppermute | solution.py:20
  30.7 2.2 %copy-start = (bf16[3,3,512,512]{3,2,1,0:T(8,128)(2,1)}, bf16[3,3,512,512]{3,2,1,0:T(8,128)(2,1)S(1)}, u32[]{:S(2)}) copy-start(bf16[3,3,512,512]{3,2,1,0:T(8,128)(2,1)S(1)} %fusion.12) | copy-start | bytes 14155780
  44.6 5.3 %copy-start.1 = (bf16[4,4,128]{2,1,0:T(4,128)(2,1)S(1)}, bf16[4,4,128]{2,1,0:T(4,128)(2,1)}, u32[]{:S(2)}) copy-start(bf16[4,4,128]{2,1,0:T(4,128)(2,1)} %param.4) | copy-start | bytes 12292
  49.9 8.0 %collective-permute-start.2 = (bf16[6,1,128]{2,1,0:T(2,128)(2,1)S(1)}, bf16[6,1,128]{2,1,0:T(2,128)(2,1)S(1)}, u32[]{:S(2)}, u32[]{:S(2)}) collective-permute-start(bf16[6,1,128]{2,1,0:T(2,128)(2,1)S(1)} %get-tuple-element.13), channel_id=1, source_target_pairs={{0,1},{1,2},{2,3},{4,5},{5,6},{6,7},{8,9},{9,10},{10,11},{12,13},{... | collective-permute-start | bytes 4616 | tf_op jit(solution)/shard_map/ppermute | solution.py:20
  54.0 4.9 %collective-permute-start.3 = (bf16[6,1,128]{2,1,0:T(2,128)(2,1)S(1)}, bf16[6,1,128]{2,1,0:T(2,128)(2,1)S(1)}, u32[]{:S(2)}, u32[]{:S(2)}) collective-permute-start(bf16[6,1,128]{2,1,0:T(2,128)(2,1)S(1)} %get-tuple-element.14), channel_id=1, source_target_pairs={{1,0},{2,1},{3,2},{5,4},{6,5},{7,6},{9,8},{10,9},{11,10},{13,12},{... | collective-permute-start | bytes 4616 | tf_op jit(solution)/shard_map/ppermute | solution.py:22
where the time goes:
time: 92.3 us; the launch traced here: 91.7 us
  local copies, waits for them, and re-layouts  52.2 us (57%)
  starting transfers between devices  17.1 us (19%)
  Pallas kernels  10.6 us (11%)
  other arithmetic  5.87 us (6%)
  matrix products  4.65 us (5%)
  waiting for transfers between devices  0.97 us (1%)
    unnamed x36, local copies, waits for them, and re-layouts  15.9 us
    ppermute x2, starting transfers between devices, extended_2(): lax.ppermute(tail, axis, [(i, (i + 1) % count) for i in range(ends)])  12.6 us
    pallas_call x1, Pallas kernels, body(): pl.pallas_call(lambda *refs: convs_kernel(width, own_rows, own_cols, *ref...  10.6 us
    transpose x1, local copies, waits for them, and re-layouts, up_tables(): up_weight.reshape(2, 4, 2, 4, 8, channels, channels)  8.3 us
    reshape x1, local copies, waits for them, and re-layouts, spread(): product = product.reshape(2, 2, 4, 4, size_one, size_two, lane_width)  6.25 us
    reshape x1, local copies, waits for them, and re-layouts, up_tables(): taps = taps.reshape(2, 2, 4, 4, channels, 8 * channels)  5.33 us
    dot_general x1, local copies, waits for them, and re-layouts, spread(): jnp.einsum('bpk,bkn->bpn', jnp.broadcast_to(flat_rows, (64,) + flat_rows....  4.96 us
    dot_general x1, matrix products, spread(): jnp.einsum('bpk,bkn->bpn', jnp.broadcast_to(flat_rows, (64,) + flat_rows....  4.65 us
  transfers between devices with their start and end apart: 4, of which 1 were waited for; matrix products, arithmetic and copies ran while one was open for 41% of the time, Pallas kernels for 0%

commit v1 on v0

v1 whole, which is shorter than its diff:
```python
import jax
import jax.numpy as jnp
import numpy as np
from jax import lax
from jax.experimental import pallas as pl
from jax.experimental.pallas import tpu as pltpu
from jax.sharding import PartitionSpec as P

HIGHEST = lax.Precision.HIGHEST


def extended_2(cells, sides, width):
    for axis, dim in sides:
        count = lax.axis_size(axis)
        ends = count - 1
        head = lax.slice_in_dim(cells, 0, width, axis=dim)
        tail = lax.slice_in_dim(cells, cells.shape[dim] - width, cells.shape[dim], axis=dim)
        cells = jnp.concatenate(
            [
                lax.ppermute(tail, axis, [(i, (i + 1) % count) for i in range(ends)]),
                cells,
                lax.ppermute(head, axis, [((i + 1) % count, i) for i in range(ends)]),
            ],
            axis=dim,
        )
    return cells


def up_tables(up_weight, coarse_depth):
    channels = up_weight.shape[3]
    fine_depth = 4 * coarse_depth
    zero = jnp.zeros((), up_weight.dtype)
    taps = up_weight.reshape(2, 4, 2, 4, 8, channels, channels).transpose(0, 2, 1, 3, 5, 4, 6)
    taps = taps.reshape(2, 2, 4, 4, channels, 8 * channels)
    keep = [(0, 0, 0)] * 5
    return jnp.concatenate(
        [
            lax.pad(
                taps,
                zero,
                keep + [(channels * (4 * c - 2), channels * (fine_depth - 4 * c - 6), 0)],
            )
            for c in range(coarse_depth)
        ],
        axis=4,
    )


def quad_band(weight):
    channels = weight.shape[3]
    zero = jnp.zeros((), weight.dtype)
    taps = weight.reshape(9, 3, channels, channels)
    keep = [(0, 0, 0)] * 2
    quads = jnp.stack(
        [lax.pad(taps, zero, [(0, 0, 0), (3 + o, 6 - o, 0)] + keep) for o in range(4)], axis=3
    )
    return quads.reshape(9, 12 * channels, 4 * channels)


def inside(axis, count, own, halo):
    place = lax.axis_index(axis)
    local = jnp.arange(count) - halo
    return ((local >= 0) | (place > 0)) & ((local < own) | (place < lax.axis_size(axis) - 1))


def fill_band(quad_ref, band_ref):
    rows = band_ref.shape[1]
    for tap in range(9):
        for group in range(rows // 128):
            low = 128 * (group - 1)
            top, bottom = max(low, 0), min(low + 384, rows)
            cols = pl.ds(128 * group, 128)
            band_ref[tap, top:bottom, cols] = quad_ref[tap, top - low : bottom - low, :]
            if top > 0:
                band_ref[tap, 0:top, cols] = jnp.zeros((top, 128), band_ref.dtype)
            if bottom < rows:
                band_ref[tap, bottom:rows, cols] = jnp.zeros((rows - bottom, 128), band_ref.dtype)


def shifted(values):
    rows = values.shape[0]
    return (
        pltpu.roll(values, 1, 0).astype(jnp.bfloat16),
        values.astype(jnp.bfloat16),
        pltpu.roll(values, rows - 1, 0).astype(jnp.bfloat16),
    )


def conv_rows(parts, band_ref, width, count):
    total = None
    for one in range(3):
        for two in range(3):
            window = parts[two][one * width : one * width + count]
            term = jnp.dot(window, band_ref[one * 3 + two], preferred_element_type=jnp.float32)
            total = term if total is None else total + term
    return total


def silu(values):
    return values / (1.0 + jnp.exp(-values))


def block_kernel(
    width, rows_out, cols_out,
    shifts_ref, up_ref, pick_ref, base_keep_ref, hidden_keep_ref, first_ref, second_ref,
    out_ref, band_ref,
):
    phases = []
    for phase in range(up_ref.shape[1]):
        total = None
        for high in range(up_ref.shape[0]):
            term = jnp.dot(shifts_ref[high], up_ref[high, phase], preferred_element_type=jnp.float32)
            total = term if total is None else total + term
        phases.append(total)
    phase_rows = silu(jnp.concatenate(phases, axis=0)).astype(jnp.bfloat16)
    base = jnp.dot(pick_ref[...], phase_rows, preferred_element_type=jnp.float32)
    base = jnp.where(base_keep_ref[...] > 0, base, 0.0)
    fill_band(first_ref, band_ref)
    hidden_count = (rows_out + 2) * width
    first = conv_rows(shifted(base), band_ref, width, hidden_count)
    hidden = jnp.where(hidden_keep_ref[...] > 0, silu(first), 0.0)
    fill_band(second_ref, band_ref)
    out_count = rows_out * width
    second = conv_rows(shifted(hidden), band_ref, width, out_count)
    summed = base[2 * width : 2 * width + out_count] + second
    summed = pltpu.roll(summed, out_count - 2, 0).reshape(rows_out, width, summed.shape[1])
    out_ref[...] = summed[:, :cols_out].astype(out_ref.dtype)


def picker(rows, cols, width, span):
    place = jnp.arange(rows * width)
    one, two = place // width, place % width
    source = ((one % 4) * 4 + two % 4) * (rows // 4) * span + (one // 4) * span + two // 4
    chosen = (jnp.arange(rows * width)[None, :] == source[:, None]) & (two < cols)[:, None]
    return chosen.astype(jnp.bfloat16)


def body(coarse_field, up_weight, first_weight, second_weight):
    channels = up_weight.shape[3]
    coarse_depth = coarse_field.shape[2] // channels
    size_one, size_two = coarse_field.shape[:2]
    own_rows, own_cols = 4 * size_one, 4 * size_two
    lanes = 4 * coarse_depth * channels
    width, span = 32, 8
    up_mats = up_tables(up_weight, coarse_depth).reshape(4, 16, coarse_depth * channels, lanes)
    coarse_ext = extended_2(coarse_field, (("strike", 0), ("dip", 1)), 1)
    shifts = jnp.stack(
        [
            jnp.pad(
                coarse_ext[1 - one : size_one + 2 - one, 1 - two : size_two + 2 - two],
                ((0, 0), (0, span - size_two - 1), (0, 0)),
            )
            for one in (0, 1)
            for two in (0, 1)
        ]
    ).reshape(4, (size_one + 1) * span, -1)
    rows_all = inside("strike", own_rows + 4, own_rows, 2)
    cols_all = inside("dip", own_cols + 4, own_cols, 2)
    cols_all = jnp.pad(cols_all, (0, width - own_cols - 4))
    base_keep = (rows_all[:, None] & cols_all[None, :]).astype(jnp.float32).reshape(-1, 1)
    position = jnp.arange(width)
    cols_hidden = cols_all & (position >= 1) & (position < own_cols + 3)
    hidden_keep = rows_all[1 : own_rows + 3, None] & cols_hidden[None, :]
    hidden_keep = hidden_keep.astype(jnp.float32).reshape(-1, 1)
    vmem = pl.BlockSpec(memory_space=pltpu.VMEM)
    return pl.pallas_call(
        lambda *refs: block_kernel(width, own_rows, own_cols, *refs),
        out_shape=jax.ShapeDtypeStruct((own_rows, own_cols, lanes), jnp.bfloat16),
        in_specs=[vmem] * 7,
        out_specs=vmem,
        scratch_shapes=[pltpu.VMEM((9, lanes, lanes), jnp.bfloat16)],
    )(
        shifts,
        up_mats,
        picker(own_rows + 4, own_cols + 4, width, span),
        base_keep,
        hidden_keep,
        quad_band(first_weight),
        quad_band(second_weight),
    )


def solution(mesh):
    return jax.shard_map(
        body,
        mesh=mesh,
        in_specs=(P("strike", "dip", None), P(), P(), P()),
        out_specs=P("strike", "dip", None),
        check_vma=False,
    )
```

time: 92.3 us -> 90.9 us (0.985)
  the two profiles are of different devices: /device:TPU:119 before, /device:TPU:193 now
where the time goes in v1:
time: 90.9 us; the launch traced here: 89.1 us
  local copies, waits for them, and re-layouts  49.6 us (55%)
  starting transfers between devices  16.2 us (18%)
  Pallas kernels  13 us (14%)
  other arithmetic  10.1 us (11%)
    another operation x4, local copies, waits for them, and re-layouts, quad_band(): jnp.stack([lax.pad(taps, zero, [(0, 0, 0), (3 + o, 6 - o, 0)] + keep) for...  19.9 us
    pallas_call x1, Pallas kernels, body(): pl.pallas_call(lambda *refs: block_kernel(width, own_rows, own_cols, *ref...  13 us
    reshape x2, local copies, waits for them, and re-layouts, quad_band(): return quads.reshape(9, 12 * channels, 4 * channels)  10.7 us
    ppermute x2, starting transfers between devices, extended_2(): lax.ppermute(head, axis, [((i + 1) % count, i) for i in range(ends)])  9.81 us
    transpose x1, local copies, waits for them, and re-layouts, up_tables(): up_weight.reshape(2, 4, 2, 4, 8, channels, channels)  8.29 us
    ppermute x2, starting transfers between devices, extended_2(): lax.ppermute(tail, axis, [(i, (i + 1) % count) for i in range(ends)])  6.39 us
    reshape x1, local copies, waits for them, and re-layouts, up_tables(): taps = taps.reshape(2, 2, 4, 4, channels, 8 * channels)  5.33 us
    concatenate x1, other arithmetic, up_tables(): jnp.concatenate([lax.pad(taps, zero, keep + [(channels * (4 * c - 2), cha...  4.37 us
  transfers between devices with their start and end apart: 4, of which 0 were waited for; matrix products, arithmetic and copies ran while one was open for 64% of the time, Pallas kernels for 0%

profile of v1, /device:TPU:193, one launch (start us, length us, event | category | flops | bytes accessed | tf_op | source)
XLA Modules:
  0.0 89.1 jit_solution(12834857656486020441)
XLA Ops:
  0.0 1.3 %fusion.48 = (bf16[1,4,128]{2,1,0:T(4,128)(2,1)}, bf16[1,4,128]{2,1,0:T(4,128)(2,1)S(1)}) fusion(bf16[4,4,128]{2,1,0:T(4,128)(2,1)} %param.4), kind=kLoop, calls=%fused_computation.96 | loop fusion | bytes 4096 | tf_op jit(solution)/shard_map/slice | solution.py:16
  1.3 3.1 %collective-permute-start = (bf16[1,4,128]{2,1,0:T(4,128)(2,1)S(1)}, bf16[1,4,128]{2,1,0:T(4,128)(2,1)S(1)}, u32[]{:S(2)}, u32[]{:S(2)}) collective-permute-start(bf16[1,4,128]{2,1,0:T(4,128)(2,1)S(1)} %get-tuple-element.22), channel_id=1, source_target_pairs={{0,4},{4,8},{8,12},{12,16},{16,20},{20,24},{24,28},{28,32},{32,36}... | collective-permute-start | bytes 3080 | tf_op jit(solution)/shard_map/ppermute | solution.py:20
  4.4 6.7 %collective-permute-start.1 = (bf16[1,4,128]{2,1,0:T(4,128)(2,1)}, bf16[1,4,128]{2,1,0:T(4,128)(2,1)S(1)}, u32[]{:S(2)}, u32[]{:S(2)}) collective-permute-start(bf16[1,4,128]{2,1,0:T(4,128)(2,1)} %get-tuple-element.21), channel_id=1, source_target_pairs={{4,0},{8,4},{12,8},{16,12},{20,16},{24,20},{28,24},{32,28},{36,32}... | collective-permute-start | bytes 3080 | tf_op jit(solution)/shard_map/ppermute | solution.py:22
  11.1 3.5 %pad_bitcast_fusion.7 = (bf16[9,12,32,1,32]{4,2,1,0,3:T(8,128)(2,1)S(1)}, bf16[9,12,32,1,32]{4,2,1,0,3:T(8,128)(2,1)S(1)}, bf16[9,12,32,1,32]{4,2,1,0,3:T(8,128)(2,1)}, bf16[9,12,32,1,32]{4,2,1,0,3:T(8,128)(2,1)}) fusion(bf16[9,3,32,32]{3,2,1,0:T(8,128)(2,1)} %bitcast.34), kind=kLoop, calls=%fused_computation.25 | loop fusion | bytes 940032 | tf_op jit(solution)/shard_map/stack | solution.py:54
  14.6 3.7 %pad_bitcast_fusion.3 = (bf16[9,12,32,1,32]{4,2,1,0,3:T(8,128)(2,1)}, bf16[9,12,32,1,32]{4,2,1,0,3:T(8,128)(2,1)}, bf16[9,12,32,1,32]{4,2,1,0,3:T(8,128)(2,1)}, bf16[9,12,32,1,32]{4,2,1,0,3:T(8,128)(2,1)}) fusion(bf16[9,3,32,32]{3,2,1,0:T(8,128)(2,1)} %bitcast.35), kind=kLoop, calls=%fused_computation.21 | loop fusion | bytes 940032 | tf_op jit(solution)/shard_map/stack | solution.py:54
  18.3 0.6 compare_and_fusion
  18.9 8.3 %copy.12 = bf16[2,2,4,4,32,8,32]{6,5,4,3,2,1,0:T(8,128)(2,1)} copy(bf16[2,2,4,4,32,8,32]{6,4,5,3,1,2,0:T(8,128)(2,1)} %bitcast.33) | data formatting | bytes 2097152 | tf_op jit(solution)/shard_map/transpose | solution.py:33
  27.2 5.3 %reshape.180 = bf16[2,2,4,4,32,256]{5,4,3,2,1,0:T(8,128)(2,1)S(1)} reshape(bf16[2,2,4,4,32,8,32]{6,5,4,3,2,1,0:T(8,128)(2,1)} %copy.12) | data formatting | bytes 2097152 | tf_op jit(solution)/shard_map/reshape | solution.py:34
  32.6 1.1 %pad_slice_fusion.1 = (bf16[2,2,4,4,32,512]{5,4,3,2,1,0:T(8,128)(2,1)S(1)}, bf16[2,2,4,4,32,512]{5,4,3,2,1,0:T(8,128)(2,1)S(1)}) fusion(bf16[2,2,4,4,32,256]{5,4,3,2,1,0:T(8,128)(2,1)S(1)} %reshape.180), kind=kLoop, calls=%fused_computation.14 | loop fusion | bytes 5242880 | tf_op jit(solution)/shard_map/pad | solution.py:38
  33.7 4.4 %fusion.5 = bf16[2,2,4,4,128,512]{5,4,3,2,1,0:T(8,128)(2,1)} fusion(bf16[2,2,4,4,32,256]{5,4,3,2,1,0:T(8,128)(2,1)S(1)} %reshape.180, bf16[2,2,4,4,32,512]{5,4,3,2,1,0:T(8,128)(2,1)S(1)} %get-tuple-element.6, bf16[2,2,4,4,32,512]{5,4,3,2,1,0:T(8,128)(2,1)S(1)} %get-tuple-element.5), kind=kLoop, calls=%fused_computation.9 | loop fusion | flops 67108864 | bytes 13631488 | tf_op jit(solution)/shard_map/concatenate | solution.py:36
  38.1 1.2 %fusion.8.refs_2_ = bf16[640,640]{1,0:T(8,128)(2,1)} fusion(s32[640]{0:T(1024)S(1)} %fusion.29, pred[640]{0:T(1024)(128)(4,1)S(1)} %fusion.32), kind=kLoop, calls=%fused_computation.17 | loop fusion | flops 1228800 | bytes 822400 | tf_op jit(solution)/shard_map/convert_element_type | solution.py:135
  39.3 1.0 %pad_maximum_fusion = bf16[9,12,32,4,32]{4,2,1,0,3:T(8,128)(2,1)S(1)} fusion(bf16[9,12,32,1,32]{4,2,1,0,3:T(8,128)(2,1)S(1)} %get-tuple-element.12, bf16[9,12,32,1,32]{4,2,1,0,3:T(8,128)(2,1)S(1)} %copy-done.4, bf16[9,12,32,1,32]{4,2,1,0,3:T(8,128)(2,1)S(1)} %copy-done.5, bf16[9,12,32,1,32]{4,2,1,0,3:T(8,128)(2,1)S(1)} %get-tuple-element.11), kind=kLoop, calls=%fused_computation.11 | loop fusion | flops 1327104 | bytes 1769472 | tf_op jit(solution)/shard_map/stack | solution.py:54
  40.3 0.0 copy-start.8
  40.3 0.0 copy-done.3
  40.4 1.0 %pad_maximum_fusion.1 = bf16[9,12,32,4,32]{4,2,1,0,3:T(8,128)(2,1)S(1)} fusion(bf16[9,12,32,1,32]{4,2,1,0,3:T(8,128)(2,1)S(1)} %copy-done.1, bf16[9,12,32,1,32]{4,2,1,0,3:T(8,128)(2,1)S(1)} %copy-done.2, bf16[9,12,32,1,32]{4,2,1,0,3:T(8,128)(2,1)S(1)} %copy-done.3, bf16[9,12,32,1,32]{4,2,1,0,3:T(8,128)(2,1)S(1)} %copy-done), kind=kLoop, calls=%fused_computation.12 | loop fusion | flops 1327104 | bytes 1769472 | tf_op jit(solution)/shard_map/stack | solution.py:54
  41.3 0.7 and_convert_fusion.1
  42.0 0.1 slice.41
  42.1 0.0 collective-permute-done.1
  42.1 0.6 fusion.47
  42.7 3.1 %collective-permute-start.2 = (bf16[6,1,128]{2,1,0:T(2,128)(2,1)}, bf16[6,1,128]{2,1,0:T(2,128)(2,1)S(1)}, u32[]{:S(2)}, u32[]{:S(2)}) collective-permute-start(bf16[6,1,128]{2,1,0:T(2,128)(2,1)} %get-tuple-element.19), channel_id=1, source_target_pairs={{1,0},{2,1},{3,2},{5,4},{6,5},{7,6},{9,8},{10,9},{11,10},{13,12},{... | collective-permute-start | bytes 4616 | tf_op jit(solution)/shard_map/ppermute | solution.py:22
  45.9 3.3 %collective-permute-start.3 = (bf16[6,1,128]{2,1,0:T(2,128)(2,1)}, bf16[6,1,128]{2,1,0:T(2,128)(2,1)S(1)}, u32[]{:S(2)}, u32[]{:S(2)}) collective-permute-start(bf16[6,1,128]{2,1,0:T(2,128)(2,1)} %get-tuple-element.20), channel_id=1, source_target_pairs={{0,1},{1,2},{2,3},{4,5},{5,6},{6,7},{8,9},{9,10},{10,11},{12,13},{... | collective-permute-start | bytes 4616 | tf_op jit(solution)/shard_map/ppermute | solution.py:20
  49.2 0.7 and_convert_fusion
  49.8 6.4 %copy.13 = bf16[9,12,32,4,32]{4,3,2,1,0:T(4,128)(2,1)} copy(bf16[9,12,32,4,32]{4,2,1,0,3:T(8,128)(2,1)S(1)} %pad_maximum_fusion) | data formatting | bytes 1769472 | tf_op jit(solution)/shard_map/stack | solution.py:54
  56.2 5.4 %reshape.183.refs_5_ = bf16[9,384,128]{2,1,0:T(8,128)(2,1)} reshape(bf16[9,12,32,4,32]{4,3,2,1,0:T(4,128)(2,1)} %copy.13) | data formatting | bytes 1769472 | tf_op jit(solution)/shard_map/reshape | solution.py:57
  61.6 6.4 %copy.14 = bf16[9,12,32,4,32]{4,3,2,1,0:T(4,128)(2,1)} copy(bf16[9,12,32,4,32]{4,2,1,0,3:T(8,128)(2,1)S(1)} %pad_maximum_fusion.1) | data formatting | bytes 1769472 | tf_op jit(solution)/shard_map/stack | solution.py:54
  67.9 5.4 %reshape.185.refs_6_ = bf16[9,384,128]{2,1,0:T(8,128)(2,1)} reshape(bf16[9,12,32,4,32]{4,3,2,1,0:T(4,128)(2,1)} %copy.14) | data formatting | bytes 1769472 | tf_op jit(solution)/shard_map/reshape | solution.py:57
  73.3 1.1 %reshape.188.refs_3_ = f32[640,1]{1,0:T(8,128)} reshape(f32[20,32]{1,0:T(8,128)S(1)} %copy-done.7) | data formatting | bytes 5120 | tf_op jit(solution)/shard_map/convert_element_type | solution.py:160
  74.4 1.0 %reshape.189.refs_4_ = f32[576,1]{1,0:T(8,128)} reshape(f32[18,32]{1,0:T(8,128)S(1)} %copy-done.6) | data formatting | bytes 4608 | tf_op jit(solution)/shard_map/convert_element_type | solution.py:164
  75.4 0.0 collective-permute-done.2
  75.4 0.0 collective-permute-done.3
  75.5 0.6 pad_maximum_fusion.2.refs_0_
  76.1 13.0 %shard_map.46 = bf16[16,16,512]{2,1,0:T(8,128)(2,1)} custom-call(bf16[4,40,128]{2,1,0:T(8,128)(2,1)} %pad_maximum_fusion.2.refs_0_, bf16[4,16,128,512]{3,2,1,0:T(8,128)(2,1)} %bitcast.32, bf16[640,640]{1,0:T(8,128)(2,1)} %fusion.8.refs_2_, f32[640,1]{1,0:T(8,128)} %reshape.188.refs_3_, f32[576,1]{1,0:T(8,128)} %reshape.189.refs_4_, ...), custom_call_target="tpu_custom_call" | custom-call | tf_op jit(solution)/shard_map/pallas_call | solution.py:166
  (29 shorter events, 0.1 us)
Async XLA Ops:
  1.3 40.8 %collective-permute-start = (bf16[1,4,128]{2,1,0:T(4,128)(2,1)S(1)}, bf16[1,4,128]{2,1,0:T(4,128)(2,1)S(1)}, u32[]{:S(2)}, u32[]{:S(2)}) collective-permute-start(bf16[1,4,128]{2,1,0:T(4,128)(2,1)S(1)} %get-tuple-element.22), channel_id=1, source_target_pairs={{0,4},{4,8},{8,12},{12,16},{16,20},{20,24},{24,28},{28,32},{32,36}... | collective-permute-start | bytes 3080 | tf_op jit(solution)/shard_map/ppermute | solution.py:20
  4.4 37.7 %collective-permute-start.1 = (bf16[1,4,128]{2,1,0:T(4,128)(2,1)}, bf16[1,4,128]{2,1,0:T(4,128)(2,1)S(1)}, u32[]{:S(2)}, u32[]{:S(2)}) collective-permute-start(bf16[1,4,128]{2,1,0:T(4,128)(2,1)} %get-tuple-element.21), channel_id=1, source_target_pairs={{4,0},{8,4},{12,8},{16,12},{20,16},{24,20},{28,24},{32,28},{36,32}... | collective-permute-start | bytes 3080 | tf_op jit(solution)/shard_map/ppermute | solution.py:22
  33.7 5.6 %copy-start.4 = (bf16[9,12,32,1,32]{4,2,1,0,3:T(8,128)(2,1)S(1)}, bf16[9,12,32,1,32]{4,2,1,0,3:T(8,128)(2,1)}, u32[]{:S(2)}) copy-start(bf16[9,12,32,1,32]{4,2,1,0,3:T(8,128)(2,1)} %get-tuple-element.13) | copy-start | bytes 663556
  33.7 5.6 %copy-start.5 = (bf16[9,12,32,1,32]{4,2,1,0,3:T(8,128)(2,1)S(1)}, bf16[9,12,32,1,32]{4,2,1,0,3:T(8,128)(2,1)}, u32[]{:S(2)}) copy-start(bf16[9,12,32,1,32]{4,2,1,0,3:T(8,128)(2,1)} %get-tuple-element.14) | copy-start | bytes 663556
  38.1 2.2 %copy-start = (bf16[9,12,32,1,32]{4,2,1,0,3:T(8,128)(2,1)S(1)}, bf16[9,12,32,1,32]{4,2,1,0,3:T(8,128)(2,1)}, u32[]{:S(2)}) copy-start(bf16[9,12,32,1,32]{4,2,1,0,3:T(8,128)(2,1)} %get-tuple-element.7) | copy-start | bytes 663556
  38.1 2.2 %copy-start.1 = (bf16[9,12,32,1,32]{4,2,1,0,3:T(8,128)(2,1)S(1)}, bf16[9,12,32,1,32]{4,2,1,0,3:T(8,128)(2,1)}, u32[]{:S(2)}) copy-start(bf16[9,12,32,1,32]{4,2,1,0,3:T(8,128)(2,1)} %get-tuple-element.8) | copy-start | bytes 663556
  38.1 2.2 %copy-start.2 = (bf16[9,12,32,1,32]{4,2,1,0,3:T(8,128)(2,1)S(1)}, bf16[9,12,32,1,32]{4,2,1,0,3:T(8,128)(2,1)}, u32[]{:S(2)}) copy-start(bf16[9,12,32,1,32]{4,2,1,0,3:T(8,128)(2,1)} %get-tuple-element.9) | copy-start | bytes 663556
  38.1 2.3 %copy-start.3 = (bf16[9,12,32,1,32]{4,2,1,0,3:T(8,128)(2,1)S(1)}, bf16[9,12,32,1,32]{4,2,1,0,3:T(8,128)(2,1)}, u32[]{:S(2)}) copy-start(bf16[9,12,32,1,32]{4,2,1,0,3:T(8,128)(2,1)} %get-tuple-element.10) | copy-start | bytes 663556
  40.3 1.8 %copy-start.8 = (bf16[4,4,128]{2,1,0:T(4,128)(2,1)S(1)}, bf16[4,4,128]{2,1,0:T(4,128)(2,1)}, u32[]{:S(2)}) copy-start(bf16[4,4,128]{2,1,0:T(4,128)(2,1)} %param.4) | copy-start | bytes 12292
  40.3 8.9 %copy-start.9 = (pred[32]{0:T(512)(128)(4,1)S(1)}, pred[32]{0:T(512)(128)(4,1)}, u32[]{:S(2)}) copy-start(pred[32]{0:T(512)(128)(4,1)} %get-tuple-element.23) | copy-start | bytes 100
  42.7 32.7 %collective-permute-start.2 = (bf16[6,1,128]{2,1,0:T(2,128)(2,1)}, bf16[6,1,128]{2,1,0:T(2,128)(2,1)S(1)}, u32[]{:S(2)}, u32[]{:S(2)}) collective-permute-start(bf16[6,1,128]{2,1,0:T(2,128)(2,1)} %get-tuple-element.19), channel_id=1, source_target_pairs={{1,0},{2,1},{3,2},{5,4},{6,5},{7,6},{9,8},{10,9},{11,10},{13,12},{... | collective-permute-start | bytes 4616 | tf_op jit(solution)/shard_map/ppermute | solution.py:22
  45.9 29.6 %collective-permute-start.3 = (bf16[6,1,128]{2,1,0:T(2,128)(2,1)}, bf16[6,1,128]{2,1,0:T(2,128)(2,1)S(1)}, u32[]{:S(2)}, u32[]{:S(2)}) collective-permute-start(bf16[6,1,128]{2,1,0:T(2,128)(2,1)} %get-tuple-element.20), channel_id=1, source_target_pairs={{0,1},{1,2},{2,3},{4,5},{5,6},{6,7},{8,9},{9,10},{10,11},{12,13},{... | collective-permute-start | bytes 4616 | tf_op jit(solution)/shard_map/ppermute | solution.py:20
  67.9 5.4 %copy-start.7 = (f32[20,32]{1,0:T(8,128)S(1)}, f32[20,32]{1,0:T(8,128)}, u32[]{:S(2)}) copy-start(f32[20,32]{1,0:T(8,128)} %and_convert_fusion.1) | copy-start | bytes 7684
  67.9 6.5 %copy-start.6 = (f32[18,32]{1,0:T(8,128)S(1)}, f32[18,32]{1,0:T(8,128)}, u32[]{:S(2)}) copy-start(f32[18,32]{1,0:T(8,128)} %and_convert_fusion) | copy-start | bytes 6916

commit v2 on v1

--- a/solution.py
+++ b/solution.py
@@ -46,35 +46,33 @@
     )
 
 
-def quad_band(weight):
-    channels = weight.shape[3]
-    zero = jnp.zeros((), weight.dtype)
-    taps = weight.reshape(9, 3, channels, channels)
-    keep = [(0, 0, 0)] * 2
-    quads = jnp.stack(
-        [lax.pad(taps, zero, [(0, 0, 0), (3 + o, 6 - o, 0)] + keep) for o in range(4)], axis=3
-    )
-    return quads.reshape(9, 12 * channels, 4 * channels)
-
-
 def inside(axis, count, own, halo):
     place = lax.axis_index(axis)
     local = jnp.arange(count) - halo
     return ((local >= 0) | (place > 0)) & ((local < own) | (place < lax.axis_size(axis) - 1))
 
 
-def fill_band(quad_ref, band_ref):
-    rows = band_ref.shape[1]
-    for tap in range(9):
-        for group in range(rows // 128):
-            low = 128 * (group - 1)
-            top, bottom = max(low, 0), min(low + 384, rows)
-            cols = pl.ds(128 * group, 128)
-            band_ref[tap, top:bottom, cols] = quad_ref[tap, top - low : bottom - low, :]
-            if top > 0:
-                band_ref[tap, 0:top, cols] = jnp.zeros((top, 128), band_ref.dtype)
-            if bottom < rows:
-                band_ref[tap, bottom:rows, cols] = jnp.zeros((rows - bottom, 128), band_ref.dtype)
+def fill_band(weight_ref, band_ref):
+    channels = weight_ref.shape[1]
+    taps = weight_ref.shape[0] // (3 * channels)
+    cells = band_ref.shape[1] // channels
+    lane = lax.broadcasted_iota(jnp.int32, (channels, 128), 1)
+    spread_out = (lane % channels == lax.broadcasted_iota(jnp.int32, (channels, 128), 0))
+    tiled = jnp.dot(weight_ref[...], spread_out.astype(weight_ref.dtype), preferred_element_type=jnp.float32)
+    quarter = lane // channels
+    per_group = 128 // channels
+    for tap in range(taps):
+        for group in range(cells // per_group):
+            for cell in range(max(0, per_group * group - 1), min(cells, per_group * group + per_group + 1)):
+                block = jnp.zeros((channels, 128), jnp.float32)
+                for out_cell in range(per_group):
+                    depth = cell - per_group * group - out_cell + 1
+                    if 0 <= depth <= 2:
+                        row = (tap * 3 + depth) * channels
+                        block = jnp.where(quarter == out_cell, tiled[row : row + channels], block)
+                band_ref[tap, pl.ds(cell * channels, channels), pl.ds(128 * group, 128)] = block.astype(
+                    band_ref.dtype
+                )
 
 
 def shifted(values):
@@ -115,6 +113,7 @@
     phase_rows = silu(jnp.concatenate(phases, axis=0)).astype(jnp.bfloat16)
     base = jnp.dot(pick_ref[...], phase_rows, preferred_element_type=jnp.float32)
     base = jnp.where(base_keep_ref[...] > 0, base, 0.0)
+    band_ref[...] = jnp.zeros(band_ref.shape, band_ref.dtype)
     fill_band(first_ref, band_ref)
     hidden_count = (rows_out + 2) * width
     first = conv_rows(shifted(base), band_ref, width, hidden_count)
@@ -175,8 +174,8 @@
         picker(own_rows + 4, own_cols + 4, width, span),
         base_keep,
         hidden_keep,
-        quad_band(first_weight),
-        quad_band(second_weight),
+        first_weight.reshape(-1, channels),
+        second_weight.reshape(-1, channels),
     )
 
 

time: 90.9 us -> 58.1 us (0.64)
  the two profiles are of different devices: /device:TPU:193 before, /device:TPU:129 now
where the time goes in v2:
time: 58.1 us; the launch traced here: 57.7 us
  local copies, waits for them, and re-layouts  19.1 us (33%)
  starting transfers between devices  17.4 us (30%)
  Pallas kernels  12.8 us (22%)
  other arithmetic  8.25 us (14%)
    pallas_call x1, Pallas kernels, body(): pl.pallas_call(lambda *refs: block_kernel(width, own_rows, own_cols, *ref...  12.8 us
    ppermute x2, starting transfers between devices, extended_2(): lax.ppermute(head, axis, [((i + 1) % count, i) for i in range(ends)])  11 us
    transpose x1, local copies, waits for them, and re-layouts, up_tables(): up_weight.reshape(2, 4, 2, 4, 8, channels, channels)  8.31 us
    ppermute x2, starting transfers between devices, extended_2(): lax.ppermute(tail, axis, [(i, (i + 1) % count) for i in range(ends)])  6.39 us
    concatenate x1, other arithmetic, up_tables(): jnp.concatenate([lax.pad(taps, zero, keep + [(channels * (4 * c - 2), cha...  6.1 us
    reshape x1, local copies, waits for them, and re-layouts, up_tables(): taps = taps.reshape(2, 2, 4, 4, channels, 8 * channels)  5.33 us
    pad x1, local copies, waits for them, and re-layouts, up_tables(): lax.pad(taps, zero, keep + [(channels * (4 * c - 2), channels * (fine_dep...  2.53 us
    convert_element_type x1, other arithmetic, picker(): return chosen.astype(jnp.bfloat16)  1.29 us
  transfers between devices with their start and end apart: 4, of which 0 were waited for; matrix products, arithmetic and copies ran while one was open for 45% of the time, Pallas kernels for 0%

profile of v2, /device:TPU:129, one launch (start us, length us, event | category | flops | bytes accessed | tf_op | source)
XLA Modules:
  0.0 57.7 jit_solution(16901175936147626140)
XLA Ops:
  0.0 0.7 %fusion.48 = (bf16[1,4,128]{2,1,0:T(4,128)(2,1)S(1)}, bf16[1,4,128]{2,1,0:T(4,128)(2,1)S(1)}) fusion(bf16[4,4,128]{2,1,0:T(4,128)(2,1)} %param.4), kind=kLoop, calls=%fused_computation.86 | loop fusion | bytes 4096 | tf_op jit(solution)/shard_map/slice | solution.py:16
  0.7 3.1 %collective-permute-start = (bf16[1,4,128]{2,1,0:T(4,128)(2,1)S(1)}, bf16[1,4,128]{2,1,0:T(4,128)(2,1)S(1)}, u32[]{:S(2)}, u32[]{:S(2)}) collective-permute-start(bf16[1,4,128]{2,1,0:T(4,128)(2,1)S(1)} %get-tuple-element.14), channel_id=1, source_target_pairs={{0,4},{4,8},{8,12},{12,16},{16,20},{20,24},{24,28},{28,32},{32,36}... | collective-permute-start | bytes 3080 | tf_op jit(solution)/shard_map/ppermute | solution.py:20
  3.8 7.9 %collective-permute-start.1 = (bf16[1,4,128]{2,1,0:T(4,128)(2,1)S(1)}, bf16[1,4,128]{2,1,0:T(4,128)(2,1)S(1)}, u32[]{:S(2)}, u32[]{:S(2)}) collective-permute-start(bf16[1,4,128]{2,1,0:T(4,128)(2,1)S(1)} %get-tuple-element.13), channel_id=1, source_target_pairs={{4,0},{8,4},{12,8},{16,12},{20,16},{24,20},{28,24},{32,28},{36,32}... | collective-permute-start | bytes 3080 | tf_op jit(solution)/shard_map/ppermute | solution.py:22
  11.7 8.3 %copy.6 = bf16[2,2,4,4,32,8,32]{6,5,4,3,2,1,0:T(8,128)(2,1)} copy(bf16[2,2,4,4,32,8,32]{6,4,5,3,1,2,0:T(8,128)(2,1)} %bitcast.17) | data formatting | bytes 2097152 | tf_op jit(solution)/shard_map/transpose | solution.py:33
  20.1 5.3 %reshape.174 = bf16[2,2,4,4,32,256]{5,4,3,2,1,0:T(8,128)(2,1)S(1)} reshape(bf16[2,2,4,4,32,8,32]{6,5,4,3,2,1,0:T(8,128)(2,1)} %copy.6) | data formatting | bytes 2097152 | tf_op jit(solution)/shard_map/reshape | solution.py:34
  25.4 2.5 %pad_slice_fusion.1 = (bf16[2,2,4,4,32,512]{5,4,3,2,1,0:T(8,128)(2,1)S(1)}, bf16[2,2,4,4,32,512]{5,4,3,2,1,0:T(8,128)(2,1)}) fusion(bf16[2,2,4,4,32,256]{5,4,3,2,1,0:T(8,128)(2,1)S(1)} %reshape.174), kind=kLoop, calls=%fused_computation.12 | loop fusion | bytes 5242880 | tf_op jit(solution)/shard_map/pad | solution.py:38
  27.9 0.0 copy-start
  28.0 6.1 %fusion.5 = bf16[2,2,4,4,128,512]{5,4,3,2,1,0:T(8,128)(2,1)} fusion(bf16[2,2,4,4,32,256]{5,4,3,2,1,0:T(8,128)(2,1)S(1)} %reshape.174, bf16[2,2,4,4,32,512]{5,4,3,2,1,0:T(8,128)(2,1)} %get-tuple-element.6, bf16[2,2,4,4,32,512]{5,4,3,2,1,0:T(8,128)(2,1)S(1)} %get-tuple-element.5), kind=kLoop, calls=%fused_computation.9 | loop fusion | flops 67108864 | bytes 13631488 | tf_op jit(solution)/shard_map/concatenate | solution.py:36
  34.1 1.3 %fusion.8.refs_2_ = bf16[640,640]{1,0:T(8,128)(2,1)} fusion(s32[640]{0:T(1024)S(1)} %fusion.29, pred[640]{0:T(1024)(128)(4,1)S(1)} %fusion.32), kind=kLoop, calls=%fused_computation.15 | loop fusion | flops 1228800 | bytes 822400 | tf_op jit(solution)/shard_map/convert_element_type | solution.py:134
  35.4 0.1 and_convert_fusion.1
  35.4 0.1 slice.41
  35.5 0.0 collective-permute-done
  35.5 0.0 copy-done
  35.5 0.0 collective-permute-done.1
  35.6 3.1 %collective-permute-start.2 = (bf16[6,1,128]{2,1,0:T(2,128)(2,1)S(1)}, bf16[6,1,128]{2,1,0:T(2,128)(2,1)S(1)}, u32[]{:S(2)}, u32[]{:S(2)}) collective-permute-start(bf16[6,1,128]{2,1,0:T(2,128)(2,1)S(1)} %get-tuple-element.11), channel_id=1, source_target_pairs={{1,0},{2,1},{3,2},{5,4},{6,5},{7,6},{9,8},{10,9},{11,10},{13,12},{... | collective-permute-start | bytes 4616 | tf_op jit(solution)/shard_map/ppermute | solution.py:22
  38.7 3.3 %collective-permute-start.3 = (bf16[6,1,128]{2,1,0:T(2,128)(2,1)S(1)}, bf16[6,1,128]{2,1,0:T(2,128)(2,1)S(1)}, u32[]{:S(2)}, u32[]{:S(2)}) collective-permute-start(bf16[6,1,128]{2,1,0:T(2,128)(2,1)S(1)} %get-tuple-element.12), channel_id=1, source_target_pairs={{0,1},{1,2},{2,3},{4,5},{5,6},{6,7},{8,9},{9,10},{10,11},{12,13},{... | collective-permute-start | bytes 4616 | tf_op jit(solution)/shard_map/ppermute | solution.py:20
  42.0 0.1 and_convert_fusion
  42.1 1.1 %reshape.180.refs_3_ = f32[640,1]{1,0:T(8,128)} reshape(f32[20,32]{1,0:T(8,128)S(1)} %and_convert_fusion.1) | data formatting | bytes 5120 | tf_op jit(solution)/shard_map/convert_element_type | solution.py:159
  43.2 1.0 %reshape.181.refs_4_ = f32[576,1]{1,0:T(8,128)} reshape(f32[18,32]{1,0:T(8,128)S(1)} %and_convert_fusion) | data formatting | bytes 4608 | tf_op jit(solution)/shard_map/convert_element_type | solution.py:163
  44.2 0.0 collective-permute-done.2
  44.2 0.0 collective-permute-done.3
  44.2 0.6 %pad_maximum_fusion.refs_0_ = bf16[4,40,128]{2,1,0:T(8,128)(2,1)} fusion(bf16[1,40,128]{2,1,0:T(8,128)(2,1)S(1)} %get-tuple-element.10, bf16[1,40,128]{2,1,0:T(8,128)(2,1)S(1)} %get-tuple-element.9, bf16[1,40,128]{2,1,0:T(8,128)(2,1)S(1)} %get-tuple-element.17, bf16[1,40,128]{2,1,0:T(8,128)(2,1)S(1)} %get-tuple-element.18), kind=kLoop, calls=%fused_computation.16 | loop fusion | flops 61440 | bytes 81920 | tf_op jit(solution)/shard_map/stack | solution.py:146
  44.9 12.8 %shard_map.46 = bf16[16,16,512]{2,1,0:T(8,128)(2,1)} custom-call(bf16[4,40,128]{2,1,0:T(8,128)(2,1)} %pad_maximum_fusion.refs_0_, bf16[4,16,128,512]{3,2,1,0:T(8,128)(2,1)} %bitcast.16, bf16[640,640]{1,0:T(8,128)(2,1)} %fusion.8.refs_2_, f32[640,1]{1,0:T(8,128)} %reshape.180.refs_3_, f32[576,1]{1,0:T(8,128)} %reshape.181.refs_4_, bf16[864,32]{1,0:T(8,128)(2,1)} %bitcast.18, ...), custom_call_target="tpu_custom_call" | custom-call | tf_op jit(solution)/shard_map/pallas_call | solution.py:165
  (12 shorter events, 0.1 us)
Async XLA Ops:
  0.7 34.8 %collective-permute-start = (bf16[1,4,128]{2,1,0:T(4,128)(2,1)S(1)}, bf16[1,4,128]{2,1,0:T(4,128)(2,1)S(1)}, u32[]{:S(2)}, u32[]{:S(2)}) collective-permute-start(bf16[1,4,128]{2,1,0:T(4,128)(2,1)S(1)} %get-tuple-element.14), channel_id=1, source_target_pairs={{0,4},{4,8},{8,12},{12,16},{16,20},{20,24},{24,28},{28,32},{32,36}... | collective-permute-start | bytes 3080 | tf_op jit(solution)/shard_map/ppermute | solution.py:20
  3.8 31.7 %collective-permute-start.1 = (bf16[1,4,128]{2,1,0:T(4,128)(2,1)S(1)}, bf16[1,4,128]{2,1,0:T(4,128)(2,1)S(1)}, u32[]{:S(2)}, u32[]{:S(2)}) collective-permute-start(bf16[1,4,128]{2,1,0:T(4,128)(2,1)S(1)} %get-tuple-element.13), channel_id=1, source_target_pairs={{4,0},{8,4},{12,8},{16,12},{20,16},{24,20},{28,24},{32,28},{36,32}... | collective-permute-start | bytes 3080 | tf_op jit(solution)/shard_map/ppermute | solution.py:22
  27.9 7.6 %copy-start = (bf16[4,4,128]{2,1,0:T(4,128)(2,1)S(1)}, bf16[4,4,128]{2,1,0:T(4,128)(2,1)}, u32[]{:S(2)}) copy-start(bf16[4,4,128]{2,1,0:T(4,128)(2,1)} %param.4) | copy-start | bytes 12292
  35.6 8.6 %collective-permute-start.2 = (bf16[6,1,128]{2,1,0:T(2,128)(2,1)S(1)}, bf16[6,1,128]{2,1,0:T(2,128)(2,1)S(1)}, u32[]{:S(2)}, u32[]{:S(2)}) collective-permute-start(bf16[6,1,128]{2,1,0:T(2,128)(2,1)S(1)} %get-tuple-element.11), channel_id=1, source_target_pairs={{1,0},{2,1},{3,2},{5,4},{6,5},{7,6},{9,8},{10,9},{11,10},{13,12},{... | collective-permute-start | bytes 4616 | tf_op jit(solution)/shard_map/ppermute | solution.py:22
  38.7 5.4 %collective-permute-start.3 = (bf16[6,1,128]{2,1,0:T(2,128)(2,1)S(1)}, bf16[6,1,128]{2,1,0:T(2,128)(2,1)S(1)}, u32[]{:S(2)}, u32[]{:S(2)}) collective-permute-start(bf16[6,1,128]{2,1,0:T(2,128)(2,1)S(1)} %get-tuple-element.12), channel_id=1, source_target_pairs={{0,1},{1,2},{2,3},{4,5},{5,6},{6,7},{8,9},{9,10},{10,11},{12,13},{... | collective-permute-start | bytes 4616 | tf_op jit(solution)/shard_map/ppermute | solution.py:20

commit v3 on v2

--- a/solution.py
+++ b/solution.py
@@ -24,26 +24,6 @@
             axis=dim,
         )
     return cells
-
-
-def up_tables(up_weight, coarse_depth):
-    channels = up_weight.shape[3]
-    fine_depth = 4 * coarse_depth
-    zero = jnp.zeros((), up_weight.dtype)
-    taps = up_weight.reshape(2, 4, 2, 4, 8, channels, channels).transpose(0, 2, 1, 3, 5, 4, 6)
-    taps = taps.reshape(2, 2, 4, 4, channels, 8 * channels)
-    keep = [(0, 0, 0)] * 5
-    return jnp.concatenate(
-        [
-            lax.pad(
-                taps,
-                zero,
-                keep + [(channels * (4 * c - 2), channels * (fine_depth - 4 * c - 6), 0)],
-            )
-            for c in range(coarse_depth)
-        ],
-        axis=4,
-    )
 
 
 def inside(axis, count, own, halo):
@@ -98,18 +78,53 @@
     return values / (1.0 + jnp.exp(-values))
 
 
+def fill_up(weight_ref, table_ref):
+    channels = weight_ref.shape[1]
+    lane = lax.broadcasted_iota(jnp.int32, (channels, 128), 1)
+    spread_out = (lane % channels == lax.broadcasted_iota(jnp.int32, (channels, 128), 0))
+    spread_out = spread_out.astype(weight_ref.dtype)
+    quarter = lane // channels
+    per_group = 128 // channels
+    span = 8 * channels
+
+    def one(taps, carry):
+        start = pl.multiple_of(taps * span, span)
+        tiled = jnp.dot(weight_ref[pl.ds(start, span)], spread_out, preferred_element_type=jnp.float32)
+        for cell in range(3):
+            block = jnp.zeros((channels, 128), jnp.float32)
+            for out_cell in range(per_group):
+                depth = 6 - 4 * cell + out_cell
+                if 0 <= depth < 8:
+                    block = jnp.where(quarter == out_cell, tiled[depth * channels : (depth + 1) * channels], block)
+            table_ref[taps, pl.ds(cell * channels, channels), :] = block.astype(table_ref.dtype)
+        return carry
+
+    lax.fori_loop(0, table_ref.shape[0], one, 0)
+
+
 def block_kernel(
     width, rows_out, cols_out,
     shifts_ref, up_ref, pick_ref, base_keep_ref, hidden_keep_ref, first_ref, second_ref,
-    out_ref, band_ref,
+    out_ref, band_ref, table_ref,
 ):
+    fill_up(up_ref, table_ref)
+    groups = 4
+    rows_in = shifts_ref.shape[1] // groups
     phases = []
-    for phase in range(up_ref.shape[1]):
-        total = None
-        for high in range(up_ref.shape[0]):
-            term = jnp.dot(shifts_ref[high], up_ref[high, phase], preferred_element_type=jnp.float32)
-            total = term if total is None else total + term
-        phases.append(total)
+    for phase_one in range(4):
+        for phase_two in range(4):
+            total = None
+            for high_one in (0, 1):
+                for high_two in (0, 1):
+                    taps = (4 * high_one + phase_one) * 8 + 4 * high_two + phase_two
+                    term = jnp.dot(
+                        shifts_ref[high_one * 2 + high_two], table_ref[taps],
+                        preferred_element_type=jnp.float32,
+                    )
+                    total = term if total is None else total + term
+            phases.append(
+                jnp.concatenate([total[g * rows_in : (g + 1) * rows_in] for g in range(groups)], axis=1)
+            )
     phase_rows = silu(jnp.concatenate(phases, axis=0)).astype(jnp.bfloat16)
     base = jnp.dot(pick_ref[...], phase_rows, preferred_element_type=jnp.float32)
     base = jnp.where(base_keep_ref[...] > 0, base, 0.0)
@@ -141,7 +156,6 @@
     own_rows, own_cols = 4 * size_one, 4 * size_two
     lanes = 4 * coarse_depth * channels
     width, span = 32, 8
-    up_mats = up_tables(up_weight, coarse_depth).reshape(4, 16, coarse_depth * channels, lanes)
     coarse_ext = extended_2(coarse_field, (("strike", 0), ("dip", 1)), 1)
     shifts = jnp.stack(
         [
@@ -153,6 +167,10 @@
             for two in (0, 1)
         ]
     ).reshape(4, (size_one + 1) * span, -1)
+    shifts = jnp.pad(shifts, ((0, 0), (0, 0), (channels, channels)))
+    shifts = jnp.stack(
+        [shifts[:, :, channels * g : channels * (g + 3)] for g in range(coarse_depth)], axis=1
+    ).reshape(4, coarse_depth * (size_one + 1) * span, 3 * channels)
     rows_all = inside("strike", own_rows + 4, own_rows, 2)
     cols_all = inside("dip", own_cols + 4, own_cols, 2)
     cols_all = jnp.pad(cols_all, (0, width - own_cols - 4))
@@ -167,10 +185,13 @@
         out_shape=jax.ShapeDtypeStruct((own_rows, own_cols, lanes), jnp.bfloat16),
         in_specs=[vmem] * 7,
         out_specs=vmem,
-        scratch_shapes=[pltpu.VMEM((9, lanes, lanes), jnp.bfloat16)],
+        scratch_shapes=[
+            pltpu.VMEM((9, lanes, lanes), jnp.bfloat16),
+            pltpu.VMEM((64, 3 * channels, 128), jnp.bfloat16),
+        ],
     )(
         shifts,
-        up_mats,
+        up_weight.reshape(-1, channels),
         picker(own_rows + 4, own_cols + 4, width, span),
         base_keep,
         hidden_keep,

time: 58.1 us -> 48 us (0.83)
  the two profiles are of different devices: /device:TPU:129 before, /device:TPU:193 now
where the time goes in v3:
time: 48 us; the launch traced here: 47.4 us
  Pallas kernels  20.4 us (42%)
  starting transfers between devices  15.6 us (32%)
  waiting for transfers between devices  5.45 us (11%)
  local copies, waits for them, and re-layouts  3.69 us (8%)
  other arithmetic  2.17 us (5%)
    pallas_call x1, Pallas kernels, body(): pl.pallas_call(lambda *refs: block_kernel(width, own_rows, own_cols, *ref...  20.4 us
    ppermute x2, starting transfers between devices, extended_2(): lax.ppermute(head, axis, [((i + 1) % count, i) for i in range(ends)])  11.5 us
    ppermute x2, waiting for transfers between devices, extended_2(): lax.ppermute(tail, axis, [(i, (i + 1) % count) for i in range(ends)])  5.44 us
    ppermute x2, starting transfers between devices, extended_2(): lax.ppermute(tail, axis, [(i, (i + 1) % count) for i in range(ends)])  4.12 us
    convert_element_type x1, other arithmetic, picker(): return chosen.astype(jnp.bfloat16)  1.22 us
    convert_element_type x1, local copies, waits for them, and re-layouts, body(): (rows_all[:, None] & cols_all[None, :]).astype(jnp.float32).reshape(-1, 1)  1.06 us
    convert_element_type x1, local copies, waits for them, and re-layouts, body(): hidden_keep = hidden_keep.astype(jnp.float32).reshape(-1, 1)  1.03 us
  transfers between devices with their start and end apart: 4, of which 1 were waited for; matrix products, arithmetic and copies ran while one was open for 9% of the time, Pallas kernels for 0%

profile of v3, /device:TPU:193, one launch (start us, length us, event | category | flops | bytes accessed | tf_op | source)
XLA Modules:
  0.0 47.4 jit_solution(14547879850066120108)
XLA Ops:
  0.0 0.7 %fusion.43 = (bf16[1,4,128]{2,1,0:T(4,128)(2,1)S(1)}, bf16[1,4,128]{2,1,0:T(4,128)(2,1)S(1)}) fusion(bf16[4,4,128]{2,1,0:T(4,128)(2,1)} %param.4), kind=kLoop, calls=%fused_computation.80 | loop fusion | bytes 4096 | tf_op jit(solution)/shard_map/slice | solution.py:16
  0.7 7.4 %collective-permute-start.1 = (bf16[1,4,128]{2,1,0:T(4,128)(2,1)S(1)}, bf16[1,4,128]{2,1,0:T(4,128)(2,1)S(1)}, u32[]{:S(2)}, u32[]{:S(2)}) collective-permute-start(bf16[1,4,128]{2,1,0:T(4,128)(2,1)S(1)} %get-tuple-element.15), channel_id=1, source_target_pairs={{4,0},{8,4},{12,8},{16,12},{20,16},{24,20},{28,24},{32,28},{36,32}... | collective-permute-start | bytes 3080 | tf_op jit(solution)/shard_map/ppermute | solution.py:22
  8.2 1.9 %collective-permute-start = (bf16[1,4,128]{2,1,0:T(4,128)(2,1)S(1)}, bf16[1,4,128]{2,1,0:T(4,128)(2,1)S(1)}, u32[]{:S(2)}, u32[]{:S(2)}) collective-permute-start(bf16[1,4,128]{2,1,0:T(4,128)(2,1)S(1)} %get-tuple-element.16), channel_id=1, source_target_pairs={{0,4},{4,8},{8,12},{12,16},{16,20},{20,24},{24,28},{28,32},{32,36}... | collective-permute-start | bytes 3080 | tf_op jit(solution)/shard_map/ppermute | solution.py:20
  10.2 1.2 %fusion.1.refs_2_ = bf16[640,640]{1,0:T(8,128)(2,1)} fusion(s32[640]{0:T(1024)S(1)} %fusion.24, pred[640]{0:T(1024)(128)(4,1)S(1)} %fusion.27), kind=kLoop, calls=%fused_computation.2 | loop fusion | flops 1228800 | bytes 822400 | tf_op jit(solution)/shard_map/convert_element_type | solution.py:149
  11.4 0.1 and_convert_fusion.1
  11.5 0.1 slice.57
  11.5 5.4 %collective-permute-done = bf16[1,4,128]{2,1,0:T(4,128)(2,1)S(1)} collective-permute-done((bf16[1,4,128]{2,1,0:T(4,128)(2,1)S(1)}, bf16[1,4,128]{2,1,0:T(4,128)(2,1)S(1)}, u32[]{:S(2)}, u32[]{:S(2)}) %collective-permute-start) | collective-permute-done | bytes 1056 | tf_op jit(solution)/shard_map/ppermute | solution.py:20
  17.0 0.7 %constant_dynamic-update-slice_fusion.1 = bf16[6,4,128]{2,1,0:T(4,128)(2,1)S(1)} fusion(bf16[6,4,128]{2,1,0:T(4,128)(2,1)S(1)} %constant_dynamic-update-slice_fusion.2, bf16[4,4,128]{2,1,0:T(4,128)(2,1)} %param.4), kind=kLoop, calls=%fused_computation.31 | loop fusion | bytes 8192
  17.7 0.0 collective-permute-done.1
  17.7 4.0 %collective-permute-start.2 = (bf16[6,1,128]{2,1,0:T(2,128)(2,1)S(1)}, bf16[6,1,128]{2,1,0:T(2,128)(2,1)S(1)}, u32[]{:S(2)}, u32[]{:S(2)}) collective-permute-start(bf16[6,1,128]{2,1,0:T(2,128)(2,1)S(1)} %get-tuple-element.13), channel_id=1, source_target_pairs={{1,0},{2,1},{3,2},{5,4},{6,5},{7,6},{9,8},{10,9},{11,10},{13,12},{... | collective-permute-start | bytes 4616 | tf_op jit(solution)/shard_map/ppermute | solution.py:22
  21.7 2.2 %collective-permute-start.3 = (bf16[6,1,128]{2,1,0:T(2,128)(2,1)S(1)}, bf16[6,1,128]{2,1,0:T(2,128)(2,1)S(1)}, u32[]{:S(2)}, u32[]{:S(2)}) collective-permute-start(bf16[6,1,128]{2,1,0:T(2,128)(2,1)S(1)} %get-tuple-element.14), channel_id=1, source_target_pairs={{0,1},{1,2},{2,3},{4,5},{5,6},{6,7},{8,9},{9,10},{10,11},{12,13},{... | collective-permute-start | bytes 4616 | tf_op jit(solution)/shard_map/ppermute | solution.py:20
  23.9 0.1 and_convert_fusion
  24.0 1.0 %reshape.177.refs_4_ = f32[576,1]{1,0:T(8,128)} reshape(f32[18,32]{1,0:T(8,128)S(1)} %and_convert_fusion) | data formatting | bytes 4608 | tf_op jit(solution)/shard_map/convert_element_type | solution.py:181
  25.0 1.1 %reshape.176.refs_3_ = f32[640,1]{1,0:T(8,128)} reshape(f32[20,32]{1,0:T(8,128)S(1)} %and_convert_fusion.1) | data formatting | bytes 5120 | tf_op jit(solution)/shard_map/convert_element_type | solution.py:177
  26.1 0.0 collective-permute-done.2
  26.1 0.0 collective-permute-done.3
  26.2 0.1 fusion.2
  26.3 0.7 %pad_maximum_fusion = bf16[4,4,40,96]{3,2,1,0:T(8,128)(2,1)} fusion(bf16[4,1,40,96]{3,2,1,0:T(8,128)(2,1)S(1)} %get-tuple-element.6, bf16[4,1,40,96]{3,2,1,0:T(8,128)(2,1)S(1)} %get-tuple-element.7, bf16[4,1,40,96]{3,2,1,0:T(8,128)(2,1)S(1)} %get-tuple-element.8, bf16[4,1,40,96]{3,2,1,0:T(8,128)(2,1)S(1)} %get-tuple-element.5), kind=kLoop, calls=%fused_computation.3 | loop fusion | flops 184320 | bytes 245760 | tf_op jit(solution)/shard_map/stack | solution.py:171
  27.0 20.4 %shard_map.46 = bf16[16,16,512]{2,1,0:T(8,128)(2,1)} custom-call(bf16[4,160,96]{2,1,0:T(8,128)(2,1)} %bitcast.27, bf16[16384,32]{1,0:T(8,128)(2,1)} %bitcast.26, bf16[640,640]{1,0:T(8,128)(2,1)} %fusion.1.refs_2_, f32[640,1]{1,0:T(8,128)} %reshape.176.refs_3_, f32[576,1]{1,0:T(8,128)} %reshape.177.refs_4_, bf16[864,32]{1,0:T(8,128)(2,1)} %bitcast.28, ...), custom_call_target="tpu_custom_call" | custom-call | tf_op jit(solution)/shard_map/pallas_call | solution.py:183
  (12 shorter events, 0.1 us)
Async XLA Ops:
  0.7 17.0 %collective-permute-start.1 = (bf16[1,4,128]{2,1,0:T(4,128)(2,1)S(1)}, bf16[1,4,128]{2,1,0:T(4,128)(2,1)S(1)}, u32[]{:S(2)}, u32[]{:S(2)}) collective-permute-start(bf16[1,4,128]{2,1,0:T(4,128)(2,1)S(1)} %get-tuple-element.15), channel_id=1, source_target_pairs={{4,0},{8,4},{12,8},{16,12},{20,16},{24,20},{28,24},{32,28},{36,32}... | collective-permute-start | bytes 3080 | tf_op jit(solution)/shard_map/ppermute | solution.py:22
  8.2 8.8 %collective-permute-start = (bf16[1,4,128]{2,1,0:T(4,128)(2,1)S(1)}, bf16[1,4,128]{2,1,0:T(4,128)(2,1)S(1)}, u32[]{:S(2)}, u32[]{:S(2)}) collective-permute-start(bf16[1,4,128]{2,1,0:T(4,128)(2,1)S(1)} %get-tuple-element.16), channel_id=1, source_target_pairs={{0,4},{4,8},{8,12},{12,16},{16,20},{20,24},{24,28},{28,32},{32,36}... | collective-permute-start | bytes 3080 | tf_op jit(solution)/shard_map/ppermute | solution.py:20
  17.7 8.4 %collective-permute-start.2 = (bf16[6,1,128]{2,1,0:T(2,128)(2,1)S(1)}, bf16[6,1,128]{2,1,0:T(2,128)(2,1)S(1)}, u32[]{:S(2)}, u32[]{:S(2)}) collective-permute-start(bf16[6,1,128]{2,1,0:T(2,128)(2,1)S(1)} %get-tuple-element.13), channel_id=1, source_target_pairs={{1,0},{2,1},{3,2},{5,4},{6,5},{7,6},{9,8},{10,9},{11,10},{13,12},{... | collective-permute-start | bytes 4616 | tf_op jit(solution)/shard_map/ppermute | solution.py:22
  21.7 4.4 %collective-permute-start.3 = (bf16[6,1,128]{2,1,0:T(2,128)(2,1)S(1)}, bf16[6,1,128]{2,1,0:T(2,128)(2,1)S(1)}, u32[]{:S(2)}, u32[]{:S(2)}) collective-permute-start(bf16[6,1,128]{2,1,0:T(2,128)(2,1)S(1)} %get-tuple-element.14), channel_id=1, source_target_pairs={{0,1},{1,2},{2,3},{4,5},{5,6},{6,7},{8,9},{9,10},{10,11},{12,13},{... | collective-permute-start | bytes 4616 | tf_op jit(solution)/shard_map/ppermute | solution.py:20

commit v4 on v3

--- a/solution.py
+++ b/solution.py
@@ -105,9 +105,9 @@
 def block_kernel(
     width, rows_out, cols_out,
     shifts_ref, up_ref, pick_ref, base_keep_ref, hidden_keep_ref, first_ref, second_ref,
-    out_ref, band_ref, table_ref,
+    out_ref, band_ref,
 ):
-    fill_up(up_ref, table_ref)
+    table_ref = up_ref
     groups = 4
     rows_in = shifts_ref.shape[1] // groups
     phases = []
@@ -156,6 +156,16 @@
     own_rows, own_cols = 4 * size_one, 4 * size_two
     lanes = 4 * coarse_depth * channels
     width, span = 32, 8
+    vmem = pl.BlockSpec(memory_space=pltpu.VMEM)
+    table = pl.pallas_call(
+        fill_up,
+        out_shape=jax.ShapeDtypeStruct((64, 3 * channels, 128), jnp.bfloat16),
+        in_specs=[vmem],
+        out_specs=vmem,
+        cost_estimate=pl.CostEstimate(
+            flops=2 * up_weight.size * 128, transcendentals=0, bytes_accessed=2 * up_weight.size + 64 * 3 * channels * 256
+        ),
+    )(up_weight.reshape(-1, channels))
     coarse_ext = extended_2(coarse_field, (("strike", 0), ("dip", 1)), 1)
     shifts = jnp.stack(
         [
@@ -187,11 +197,10 @@
         out_specs=vmem,
         scratch_shapes=[
             pltpu.VMEM((9, lanes, lanes), jnp.bfloat16),
-            pltpu.VMEM((64, 3 * channels, 128), jnp.bfloat16),
         ],
     )(
         shifts,
-        up_weight.reshape(-1, channels),
+        table,
         picker(own_rows + 4, own_cols + 4, width, span),
         base_keep,
         hidden_keep,

time: 48 us -> 50.5 us (1.052)
  Pallas kernels: 20.4 us -> 22.9 us
    pallas_call x0 -> x1, Pallas kernels: none -> 12.5 us  [body(): pl.pallas_call(fill_up, out_shape=jax.ShapeDtypeStruct((64, 3 * channels,...]
    pallas_call x1, Pallas kernels: 20.4 us -> 10.4 us  [body(): pl.pallas_call(lambda *refs: block_kernel(width, own_rows, own_cols, *ref...]
  transfers between devices with their start and end apart: 4 -> 4, of which waited for: 1 -> 1; matrix products, arithmetic and copies ran while one was open for 9% -> 9% of each run, Pallas kernels for 0% -> 25%
where the time goes in v4:
time: 50.5 us; the launch traced here: 49.9 us
  Pallas kernels  22.9 us (45%)
  starting transfers between devices  15.6 us (31%)
  waiting for transfers between devices  5.39 us (11%)
  local copies, waits for them, and re-layouts  3.69 us (7%)
  other arithmetic  2.17 us (4%)
    pallas_call x1, Pallas kernels, body(): pl.pallas_call(fill_up, out_shape=jax.ShapeDtypeStruct((64, 3 * channels,...  12.5 us
    ppermute x2, starting transfers between devices, extended_2(): lax.ppermute(head, axis, [((i + 1) % count, i) for i in range(ends)])  11.5 us
    pallas_call x1, Pallas kernels, body(): pl.pallas_call(lambda *refs: block_kernel(width, own_rows, own_cols, *ref...  10.4 us
    ppermute x2, waiting for transfers between devices, extended_2(): lax.ppermute(tail, axis, [(i, (i + 1) % count) for i in range(ends)])  5.39 us
    ppermute x2, starting transfers between devices, extended_2(): lax.ppermute(tail, axis, [(i, (i + 1) % count) for i in range(ends)])  4.12 us
    convert_element_type x1, other arithmetic, picker(): return chosen.astype(jnp.bfloat16)  1.21 us
    convert_element_type x1, local copies, waits for them, and re-layouts, body(): (rows_all[:, None] & cols_all[None, :]).astype(jnp.float32).reshape(-1, 1)  1.06 us
    convert_element_type x1, local copies, waits for them, and re-layouts, body(): hidden_keep = hidden_keep.astype(jnp.float32).reshape(-1, 1)  1.03 us
  transfers between devices with their start and end apart: 4, of which 1 were waited for; matrix products, arithmetic and copies ran while one was open for 9% of the time, Pallas kernels for 25%

profile of v4, /device:TPU:193, one launch (start us, length us, event | category | flops | bytes accessed | tf_op | source)
XLA Modules:
  0.0 49.9 jit_solution(17831219329714714429)
XLA Ops:
  0.0 0.7 %fusion.43 = (bf16[1,4,128]{2,1,0:T(4,128)(2,1)S(1)}, bf16[1,4,128]{2,1,0:T(4,128)(2,1)S(1)}) fusion(bf16[4,4,128]{2,1,0:T(4,128)(2,1)} %param.4), kind=kLoop, calls=%fused_computation.80 | loop fusion | bytes 4096 | tf_op jit(solution)/shard_map/slice | solution.py:16
  0.7 7.4 %collective-permute-start.1 = (bf16[1,4,128]{2,1,0:T(4,128)(2,1)S(1)}, bf16[1,4,128]{2,1,0:T(4,128)(2,1)S(1)}, u32[]{:S(2)}, u32[]{:S(2)}) collective-permute-start(bf16[1,4,128]{2,1,0:T(4,128)(2,1)S(1)} %get-tuple-element.15), channel_id=1, source_target_pairs={{4,0},{8,4},{12,8},{16,12},{20,16},{24,20},{28,24},{32,28},{36,32}... | collective-permute-start | bytes 3080 | tf_op jit(solution)/shard_map/ppermute | solution.py:22
  8.2 1.9 %collective-permute-start = (bf16[1,4,128]{2,1,0:T(4,128)(2,1)S(1)}, bf16[1,4,128]{2,1,0:T(4,128)(2,1)S(1)}, u32[]{:S(2)}, u32[]{:S(2)}) collective-permute-start(bf16[1,4,128]{2,1,0:T(4,128)(2,1)S(1)} %get-tuple-element.16), channel_id=1, source_target_pairs={{0,4},{4,8},{8,12},{12,16},{16,20},{20,24},{24,28},{28,32},{32,36}... | collective-permute-start | bytes 3080 | tf_op jit(solution)/shard_map/ppermute | solution.py:20
  10.1 0.1 slice.57
  10.2 0.1 and_convert_fusion.1
  10.3 1.2 %fusion.1.refs_2_ = bf16[640,640]{1,0:T(8,128)(2,1)} fusion(s32[640]{0:T(1024)S(1)} %fusion.24, pred[640]{0:T(1024)(128)(4,1)S(1)} %fusion.27), kind=kLoop, calls=%fused_computation.2 | loop fusion | flops 1228800 | bytes 822400 | tf_op jit(solution)/shard_map/convert_element_type | solution.py:149
  11.5 0.1 and_convert_fusion
  11.6 5.4 %collective-permute-done = bf16[1,4,128]{2,1,0:T(4,128)(2,1)S(1)} collective-permute-done((bf16[1,4,128]{2,1,0:T(4,128)(2,1)S(1)}, bf16[1,4,128]{2,1,0:T(4,128)(2,1)S(1)}, u32[]{:S(2)}, u32[]{:S(2)}) %collective-permute-start) | collective-permute-done | bytes 1056 | tf_op jit(solution)/shard_map/ppermute | solution.py:20
  17.0 0.7 %constant_dynamic-update-slice_fusion.1 = bf16[6,4,128]{2,1,0:T(4,128)(2,1)S(1)} fusion(bf16[6,4,128]{2,1,0:T(4,128)(2,1)S(1)} %constant_dynamic-update-slice_fusion.2, bf16[4,4,128]{2,1,0:T(4,128)(2,1)} %param.4), kind=kLoop, calls=%fused_computation.31 | loop fusion | bytes 8192
  17.7 0.0 collective-permute-done.1
  17.7 4.0 %collective-permute-start.2 = (bf16[6,1,128]{2,1,0:T(2,128)(2,1)S(1)}, bf16[6,1,128]{2,1,0:T(2,128)(2,1)S(1)}, u32[]{:S(2)}, u32[]{:S(2)}) collective-permute-start(bf16[6,1,128]{2,1,0:T(2,128)(2,1)S(1)} %get-tuple-element.13), channel_id=1, source_target_pairs={{1,0},{2,1},{3,2},{5,4},{6,5},{7,6},{9,8},{10,9},{11,10},{13,12},{... | collective-permute-start | bytes 4616 | tf_op jit(solution)/shard_map/ppermute | solution.py:22
  21.7 2.2 %collective-permute-start.3 = (bf16[6,1,128]{2,1,0:T(2,128)(2,1)S(1)}, bf16[6,1,128]{2,1,0:T(2,128)(2,1)S(1)}, u32[]{:S(2)}, u32[]{:S(2)}) collective-permute-start(bf16[6,1,128]{2,1,0:T(2,128)(2,1)S(1)} %get-tuple-element.14), channel_id=1, source_target_pairs={{0,1},{1,2},{2,3},{4,5},{5,6},{6,7},{8,9},{9,10},{10,11},{12,13},{... | collective-permute-start | bytes 4616 | tf_op jit(solution)/shard_map/ppermute | solution.py:20
  23.9 12.5 %shard_map.46.refs_1_ = bf16[64,96,128]{2,1,0:T(8,128)(2,1)} custom-call(bf16[16384,32]{1,0:T(8,128)(2,1)} %bitcast.26), custom_call_target="tpu_custom_call" | custom-call | flops 134217728 | bytes 2621440 | tf_op jit(solution)/shard_map/pallas_call | solution.py:160
  36.4 1.0 %reshape.177.refs_4_ = f32[576,1]{1,0:T(8,128)} reshape(f32[18,32]{1,0:T(8,128)S(1)} %and_convert_fusion) | data formatting | bytes 4608 | tf_op jit(solution)/shard_map/convert_element_type | solution.py:191
  37.5 1.1 %reshape.176.refs_3_ = f32[640,1]{1,0:T(8,128)} reshape(f32[20,32]{1,0:T(8,128)S(1)} %and_convert_fusion.1) | data formatting | bytes 5120 | tf_op jit(solution)/shard_map/convert_element_type | solution.py:187
  38.5 0.0 collective-permute-done.2
  38.5 0.0 collective-permute-done.3
  38.6 0.1 fusion.2
  38.7 0.7 %pad_maximum_fusion = bf16[4,4,40,96]{3,2,1,0:T(8,128)(2,1)} fusion(bf16[4,1,40,96]{3,2,1,0:T(8,128)(2,1)S(1)} %get-tuple-element.6, bf16[4,1,40,96]{3,2,1,0:T(8,128)(2,1)S(1)} %get-tuple-element.7, bf16[4,1,40,96]{3,2,1,0:T(8,128)(2,1)S(1)} %get-tuple-element.8, bf16[4,1,40,96]{3,2,1,0:T(8,128)(2,1)S(1)} %get-tuple-element.5), kind=kLoop, calls=%fused_computation.3 | loop fusion | flops 184320 | bytes 245760 | tf_op jit(solution)/shard_map/stack | solution.py:181
  39.5 10.4 %shard_map.47 = bf16[16,16,512]{2,1,0:T(8,128)(2,1)} custom-call(bf16[4,160,96]{2,1,0:T(8,128)(2,1)} %bitcast.27, bf16[64,96,128]{2,1,0:T(8,128)(2,1)} %shard_map.46.refs_1_, bf16[640,640]{1,0:T(8,128)(2,1)} %fusion.1.refs_2_, f32[640,1]{1,0:T(8,128)} %reshape.176.refs_3_, f32[576,1]{1,0:T(8,128)} %reshape.177.refs_4_, bf16[864,32]{1,0:T(8,128)(2,1)} %bitcast.28, ...), custom_call_target="tpu_custom_call" | custom-call | tf_op jit(solution)/shard_map/pallas_call | solution.py:193
  (12 shorter events, 0.1 us)
Async XLA Ops:
  0.7 17.0 %collective-permute-start.1 = (bf16[1,4,128]{2,1,0:T(4,128)(2,1)S(1)}, bf16[1,4,128]{2,1,0:T(4,128)(2,1)S(1)}, u32[]{:S(2)}, u32[]{:S(2)}) collective-permute-start(bf16[1,4,128]{2,1,0:T(4,128)(2,1)S(1)} %get-tuple-element.15), channel_id=1, source_target_pairs={{4,0},{8,4},{12,8},{16,12},{20,16},{24,20},{28,24},{32,28},{36,32}... | collective-permute-start | bytes 3080 | tf_op jit(solution)/shard_map/ppermute | solution.py:22
  8.2 8.8 %collective-permute-start = (bf16[1,4,128]{2,1,0:T(4,128)(2,1)S(1)}, bf16[1,4,128]{2,1,0:T(4,128)(2,1)S(1)}, u32[]{:S(2)}, u32[]{:S(2)}) collective-permute-start(bf16[1,4,128]{2,1,0:T(4,128)(2,1)S(1)} %get-tuple-element.16), channel_id=1, source_target_pairs={{0,4},{4,8},{8,12},{12,16},{16,20},{20,24},{24,28},{28,32},{32,36}... | collective-permute-start | bytes 3080 | tf_op jit(solution)/shard_map/ppermute | solution.py:20
  17.7 20.8 %collective-permute-start.2 = (bf16[6,1,128]{2,1,0:T(2,128)(2,1)S(1)}, bf16[6,1,128]{2,1,0:T(2,128)(2,1)S(1)}, u32[]{:S(2)}, u32[]{:S(2)}) collective-permute-start(bf16[6,1,128]{2,1,0:T(2,128)(2,1)S(1)} %get-tuple-element.13), channel_id=1, source_target_pairs={{1,0},{2,1},{3,2},{5,4},{6,5},{7,6},{9,8},{10,9},{11,10},{13,12},{... | collective-permute-start | bytes 4616 | tf_op jit(solution)/shard_map/ppermute | solution.py:22
  21.7 16.8 %collective-permute-start.3 = (bf16[6,1,128]{2,1,0:T(2,128)(2,1)S(1)}, bf16[6,1,128]{2,1,0:T(2,128)(2,1)S(1)}, u32[]{:S(2)}, u32[]{:S(2)}) collective-permute-start(bf16[6,1,128]{2,1,0:T(2,128)(2,1)S(1)} %get-tuple-element.14), channel_id=1, source_target_pairs={{0,1},{1,2},{2,3},{4,5},{5,6},{6,7},{8,9},{9,10},{10,11},{12,13},{... | collective-permute-start | bytes 4616 | tf_op jit(solution)/shard_map/ppermute | solution.py:20

commit v5 on v3

--- a/solution.py
+++ b/solution.py
@@ -87,19 +87,27 @@
     per_group = 128 // channels
     span = 8 * channels
 
-    def one(taps, carry):
-        start = pl.multiple_of(taps * span, span)
-        tiled = jnp.dot(weight_ref[pl.ds(start, span)], spread_out, preferred_element_type=jnp.float32)
-        for cell in range(3):
-            block = jnp.zeros((channels, 128), jnp.float32)
-            for out_cell in range(per_group):
-                depth = 6 - 4 * cell + out_cell
-                if 0 <= depth < 8:
-                    block = jnp.where(quarter == out_cell, tiled[depth * channels : (depth + 1) * channels], block)
-            table_ref[taps, pl.ds(cell * channels, channels), :] = block.astype(table_ref.dtype)
+    chunk = 8
+
+    def one(step, carry):
+        start = pl.multiple_of(step * chunk * span, chunk * span)
+        tiled = jnp.dot(
+            weight_ref[pl.ds(start, chunk * span)], spread_out, preferred_element_type=jnp.float32
+        )
+        for part in range(chunk):
+            for cell in range(3):
+                block = jnp.zeros((channels, 128), jnp.float32)
+                for out_cell in range(per_group):
+                    depth = 6 - 4 * cell + out_cell
+                    if 0 <= depth < 8:
+                        row = part * span + depth * channels
+                        block = jnp.where(quarter == out_cell, tiled[row : row + channels], block)
+                table_ref[step * chunk + part, pl.ds(cell * channels, channels), :] = block.astype(
+                    table_ref.dtype
+                )
         return carry
 
-    lax.fori_loop(0, table_ref.shape[0], one, 0)
+    lax.fori_loop(0, table_ref.shape[0] // chunk, one, 0)
 
 
 def block_kernel(

time: 48 us -> 41 us (0.85)
  Pallas kernels: 20.4 us -> 13.4 us
    pallas_call x1, Pallas kernels: 20.4 us -> 13.4 us  [body(): pl.pallas_call(lambda *refs: block_kernel(width, own_rows, own_cols, *ref...]
  transfers between devices with their start and end apart: 4 -> 4, of which waited for: 1 -> 1; matrix products, arithmetic and copies ran while one was open for 9% -> 11% of each run, Pallas kernels for 0% -> 0%
where the time goes in v5:
time: 41 us; the launch traced here: 40.4 us
  starting transfers between devices  15.6 us (38%)
  Pallas kernels  13.4 us (33%)
  waiting for transfers between devices  5.45 us (13%)
  local copies, waits for them, and re-layouts  3.69 us (9%)
  other arithmetic  2.17 us (5%)
    pallas_call x1, Pallas kernels, body(): pl.pallas_call(lambda *refs: block_kernel(width, own_rows, own_cols, *ref...  13.4 us
    ppermute x2, starting transfers between devices, extended_2(): lax.ppermute(head, axis, [((i + 1) % count, i) for i in range(ends)])  11.5 us
    ppermute x2, waiting for transfers between devices, extended_2(): lax.ppermute(tail, axis, [(i, (i + 1) % count) for i in range(ends)])  5.44 us
    ppermute x2, starting transfers between devices, extended_2(): lax.ppermute(tail, axis, [(i, (i + 1) % count) for i in range(ends)])  4.12 us
    convert_element_type x1, other arithmetic, picker(): return chosen.astype(jnp.bfloat16)  1.22 us
    convert_element_type x1, local copies, waits for them, and re-layouts, body(): (rows_all[:, None] & cols_all[None, :]).astype(jnp.float32).reshape(-1, 1)  1.06 us
    convert_element_type x1, local copies, waits for them, and re-layouts, body(): hidden_keep = hidden_keep.astype(jnp.float32).reshape(-1, 1)  1.03 us
  transfers between devices with their start and end apart: 4, of which 1 were waited for; matrix products, arithmetic and copies ran while one was open for 11% of the time, Pallas kernels for 0%

profile of v5, /device:TPU:193, one launch (start us, length us, event | category | flops | bytes accessed | tf_op | source)
XLA Modules:
  0.0 40.4 jit_solution(2547258357556567414)
XLA Ops:
  0.0 0.7 %fusion.43 = (bf16[1,4,128]{2,1,0:T(4,128)(2,1)S(1)}, bf16[1,4,128]{2,1,0:T(4,128)(2,1)S(1)}) fusion(bf16[4,4,128]{2,1,0:T(4,128)(2,1)} %param.4), kind=kLoop, calls=%fused_computation.80 | loop fusion | bytes 4096 | tf_op jit(solution)/shard_map/slice | solution.py:16
  0.7 7.4 %collective-permute-start.1 = (bf16[1,4,128]{2,1,0:T(4,128)(2,1)S(1)}, bf16[1,4,128]{2,1,0:T(4,128)(2,1)S(1)}, u32[]{:S(2)}, u32[]{:S(2)}) collective-permute-start(bf16[1,4,128]{2,1,0:T(4,128)(2,1)S(1)} %get-tuple-element.15), channel_id=1, source_target_pairs={{4,0},{8,4},{12,8},{16,12},{20,16},{24,20},{28,24},{32,28},{36,32}... | collective-permute-start | bytes 3080 | tf_op jit(solution)/shard_map/ppermute | solution.py:22
  8.2 1.9 %collective-permute-start = (bf16[1,4,128]{2,1,0:T(4,128)(2,1)S(1)}, bf16[1,4,128]{2,1,0:T(4,128)(2,1)S(1)}, u32[]{:S(2)}, u32[]{:S(2)}) collective-permute-start(bf16[1,4,128]{2,1,0:T(4,128)(2,1)S(1)} %get-tuple-element.16), channel_id=1, source_target_pairs={{0,4},{4,8},{8,12},{12,16},{16,20},{20,24},{24,28},{28,32},{32,36}... | collective-permute-start | bytes 3080 | tf_op jit(solution)/shard_map/ppermute | solution.py:20
  10.2 1.2 %fusion.1.refs_2_ = bf16[640,640]{1,0:T(8,128)(2,1)} fusion(s32[640]{0:T(1024)S(1)} %fusion.24, pred[640]{0:T(1024)(128)(4,1)S(1)} %fusion.27), kind=kLoop, calls=%fused_computation.2 | loop fusion | flops 1228800 | bytes 822400 | tf_op jit(solution)/shard_map/convert_element_type | solution.py:157
  11.4 0.1 and_convert_fusion.1
  11.5 0.1 slice.57
  11.5 5.4 %collective-permute-done = bf16[1,4,128]{2,1,0:T(4,128)(2,1)S(1)} collective-permute-done((bf16[1,4,128]{2,1,0:T(4,128)(2,1)S(1)}, bf16[1,4,128]{2,1,0:T(4,128)(2,1)S(1)}, u32[]{:S(2)}, u32[]{:S(2)}) %collective-permute-start) | collective-permute-done | bytes 1056 | tf_op jit(solution)/shard_map/ppermute | solution.py:20
  17.0 0.7 %constant_dynamic-update-slice_fusion.1 = bf16[6,4,128]{2,1,0:T(4,128)(2,1)S(1)} fusion(bf16[6,4,128]{2,1,0:T(4,128)(2,1)S(1)} %constant_dynamic-update-slice_fusion.2, bf16[4,4,128]{2,1,0:T(4,128)(2,1)} %param.4), kind=kLoop, calls=%fused_computation.31 | loop fusion | bytes 8192
  17.7 0.0 collective-permute-done.1
  17.7 4.0 %collective-permute-start.2 = (bf16[6,1,128]{2,1,0:T(2,128)(2,1)S(1)}, bf16[6,1,128]{2,1,0:T(2,128)(2,1)S(1)}, u32[]{:S(2)}, u32[]{:S(2)}) collective-permute-start(bf16[6,1,128]{2,1,0:T(2,128)(2,1)S(1)} %get-tuple-element.13), channel_id=1, source_target_pairs={{1,0},{2,1},{3,2},{5,4},{6,5},{7,6},{9,8},{10,9},{11,10},{13,12},{... | collective-permute-start | bytes 4616 | tf_op jit(solution)/shard_map/ppermute | solution.py:22
  21.7 2.2 %collective-permute-start.3 = (bf16[6,1,128]{2,1,0:T(2,128)(2,1)S(1)}, bf16[6,1,128]{2,1,0:T(2,128)(2,1)S(1)}, u32[]{:S(2)}, u32[]{:S(2)}) collective-permute-start(bf16[6,1,128]{2,1,0:T(2,128)(2,1)S(1)} %get-tuple-element.14), channel_id=1, source_target_pairs={{0,1},{1,2},{2,3},{4,5},{5,6},{6,7},{8,9},{9,10},{10,11},{12,13},{... | collective-permute-start | bytes 4616 | tf_op jit(solution)/shard_map/ppermute | solution.py:20
  23.9 0.1 and_convert_fusion
  24.0 1.0 %reshape.177.refs_4_ = f32[576,1]{1,0:T(8,128)} reshape(f32[18,32]{1,0:T(8,128)S(1)} %and_convert_fusion) | data formatting | bytes 4608 | tf_op jit(solution)/shard_map/convert_element_type | solution.py:189
  25.0 1.1 %reshape.176.refs_3_ = f32[640,1]{1,0:T(8,128)} reshape(f32[20,32]{1,0:T(8,128)S(1)} %and_convert_fusion.1) | data formatting | bytes 5120 | tf_op jit(solution)/shard_map/convert_element_type | solution.py:185
  26.1 0.0 collective-permute-done.2
  26.1 0.0 collective-permute-done.3
  26.2 0.1 fusion.2
  26.3 0.7 %pad_maximum_fusion = bf16[4,4,40,96]{3,2,1,0:T(8,128)(2,1)} fusion(bf16[4,1,40,96]{3,2,1,0:T(8,128)(2,1)S(1)} %get-tuple-element.6, bf16[4,1,40,96]{3,2,1,0:T(8,128)(2,1)S(1)} %get-tuple-element.7, bf16[4,1,40,96]{3,2,1,0:T(8,128)(2,1)S(1)} %get-tuple-element.8, bf16[4,1,40,96]{3,2,1,0:T(8,128)(2,1)S(1)} %get-tuple-element.5), kind=kLoop, calls=%fused_computation.3 | loop fusion | flops 184320 | bytes 245760 | tf_op jit(solution)/shard_map/stack | solution.py:179
  27.0 13.4 %shard_map.46 = bf16[16,16,512]{2,1,0:T(8,128)(2,1)} custom-call(bf16[4,160,96]{2,1,0:T(8,128)(2,1)} %bitcast.27, bf16[16384,32]{1,0:T(8,128)(2,1)} %bitcast.26, bf16[640,640]{1,0:T(8,128)(2,1)} %fusion.1.refs_2_, f32[640,1]{1,0:T(8,128)} %reshape.176.refs_3_, f32[576,1]{1,0:T(8,128)} %reshape.177.refs_4_, bf16[864,32]{1,0:T(8,128)(2,1)} %bitcast.28, ...), custom_call_target="tpu_custom_call" | custom-call | tf_op jit(solution)/shard_map/pallas_call | solution.py:191
  (12 shorter events, 0.1 us)
Async XLA Ops:
  0.7 17.0 %collective-permute-start.1 = (bf16[1,4,128]{2,1,0:T(4,128)(2,1)S(1)}, bf16[1,4,128]{2,1,0:T(4,128)(2,1)S(1)}, u32[]{:S(2)}, u32[]{:S(2)}) collective-permute-start(bf16[1,4,128]{2,1,0:T(4,128)(2,1)S(1)} %get-tuple-element.15), channel_id=1, source_target_pairs={{4,0},{8,4},{12,8},{16,12},{20,16},{24,20},{28,24},{32,28},{36,32}... | collective-permute-start | bytes 3080 | tf_op jit(solution)/shard_map/ppermute | solution.py:22
  8.2 8.8 %collective-permute-start = (bf16[1,4,128]{2,1,0:T(4,128)(2,1)S(1)}, bf16[1,4,128]{2,1,0:T(4,128)(2,1)S(1)}, u32[]{:S(2)}, u32[]{:S(2)}) collective-permute-start(bf16[1,4,128]{2,1,0:T(4,128)(2,1)S(1)} %get-tuple-element.16), channel_id=1, source_target_pairs={{0,4},{4,8},{8,12},{12,16},{16,20},{20,24},{24,28},{28,32},{32,36}... | collective-permute-start | bytes 3080 | tf_op jit(solution)/shard_map/ppermute | solution.py:20
  17.7 8.4 %collective-permute-start.2 = (bf16[6,1,128]{2,1,0:T(2,128)(2,1)S(1)}, bf16[6,1,128]{2,1,0:T(2,128)(2,1)S(1)}, u32[]{:S(2)}, u32[]{:S(2)}) collective-permute-start(bf16[6,1,128]{2,1,0:T(2,128)(2,1)S(1)} %get-tuple-element.13), channel_id=1, source_target_pairs={{1,0},{2,1},{3,2},{5,4},{6,5},{7,6},{9,8},{10,9},{11,10},{13,12},{... | collective-permute-start | bytes 4616 | tf_op jit(solution)/shard_map/ppermute | solution.py:22
  21.7 4.4 %collective-permute-start.3 = (bf16[6,1,128]{2,1,0:T(2,128)(2,1)S(1)}, bf16[6,1,128]{2,1,0:T(2,128)(2,1)S(1)}, u32[]{:S(2)}, u32[]{:S(2)}) collective-permute-start(bf16[6,1,128]{2,1,0:T(2,128)(2,1)S(1)} %get-tuple-element.14), channel_id=1, source_target_pairs={{0,1},{1,2},{2,3},{4,5},{5,6},{6,7},{8,9},{9,10},{10,11},{12,13},{... | collective-permute-start | bytes 4616 | tf_op jit(solution)/shard_map/ppermute | solution.py:20

commit v6 on v5

--- a/solution.py
+++ b/solution.py
@@ -7,23 +7,6 @@
 from jax.sharding import PartitionSpec as P
 
 HIGHEST = lax.Precision.HIGHEST
-
-
-def extended_2(cells, sides, width):
-    for axis, dim in sides:
-        count = lax.axis_size(axis)
-        ends = count - 1
-        head = lax.slice_in_dim(cells, 0, width, axis=dim)
-        tail = lax.slice_in_dim(cells, cells.shape[dim] - width, cells.shape[dim], axis=dim)
-        cells = jnp.concatenate(
-            [
-                lax.ppermute(tail, axis, [(i, (i + 1) % count) for i in range(ends)]),
-                cells,
-                lax.ppermute(head, axis, [((i + 1) % count, i) for i in range(ends)]),
-            ],
-            axis=dim,
-        )
-    return cells
 
 
 def inside(axis, count, own, halo):
@@ -95,6 +78,9 @@
             weight_ref[pl.ds(start, chunk * span)], spread_out, preferred_element_type=jnp.float32
         )
         for part in range(chunk):
+            table_ref[step * chunk + part, pl.ds(3 * channels, channels), :] = jnp.zeros(
+                (channels, 128), table_ref.dtype
+            )
             for cell in range(3):
                 block = jnp.zeros((channels, 128), jnp.float32)
                 for out_cell in range(per_group):
@@ -110,14 +96,107 @@
     lax.fori_loop(0, table_ref.shape[0] // chunk, one, 0)
 
 
+DIRECTIONS = [(-1, -1), (-1, 0), (-1, 1), (0, -1), (0, 1), (1, -1), (1, 0), (1, 1)]
+
+
+def halo_rows(own_ref, staging_ref, size_one):
+    sub = lax.broadcasted_iota(jnp.int32, own_ref.shape[1:], 0)
+
+    def block_row(one, two, row):
+        if (one, two) == (0, 0):
+            return own_ref[row]
+        return staging_ref[DIRECTIONS.index((one, two)), row]
+
+    rows = []
+    for ext in range(size_one + 2):
+        one = -1 if ext == 0 else (1 if ext == size_one + 1 else 0)
+        row = size_one - 1 if ext == 0 else (0 if ext == size_one + 1 else ext - 1)
+        left = pltpu.roll(block_row(one, -1, row), 5, 0)
+        middle = pltpu.roll(block_row(one, 0, row), 1, 0)
+        right = pltpu.roll(block_row(one, 1, row), 5, 0)
+        value = jnp.where(sub == 5, right, 0.0)
+        value = jnp.where((sub >= 1) & (sub <= 4), middle, value)
+        rows.append(jnp.where(sub == 0, left, value))
+    return rows
+
+
 def block_kernel(
-    width, rows_out, cols_out,
-    shifts_ref, up_ref, pick_ref, base_keep_ref, hidden_keep_ref, first_ref, second_ref,
-    out_ref, band_ref, table_ref,
+    width, rows_out, cols_out, grid_shape,
+    own_ref, up_ref, pick_ref, base_keep_ref, hidden_keep_ref, first_ref, second_ref,
+    out_ref, band_ref, table_ref, staging_ref, send_sems, recv_sems,
 ):
+    place = (lax.axis_index("strike"), lax.axis_index("dip"))
+    present = [
+        (place[0] + one >= 0) & (place[0] + one < grid_shape[0]) & (place[1] + two >= 0) & (place[1] + two < grid_shape[1])
+        for one, two in DIRECTIONS
+    ]
+    for slot in range(len(DIRECTIONS)):
+        @pl.when(jnp.logical_not(present[slot]))
+        def _():
+            staging_ref[slot] = jnp.zeros(staging_ref.shape[1:], staging_ref.dtype)
+
+    barrier = pltpu.get_barrier_semaphore()
+    for slot, (one, two) in enumerate(DIRECTIONS):
+        @pl.when(present[slot])
+        def _():
+            pl.semaphore_signal(
+                barrier, 1, device_id=(place[0] + one, place[1] + two),
+                device_id_type=pl.DeviceIdType.MESH,
+            )
+    count = sum(p.astype(jnp.int32) for p in present)
+    pl.semaphore_wait(barrier, count)
+
+    copies = []
+    for slot, (one, two) in enumerate(DIRECTIONS):
+        far = len(DIRECTIONS) - 1 - slot
+        copy = pltpu.make_async_remote_copy(
+            src_ref=own_ref, dst_ref=staging_ref.at[far], send_sem=send_sems.at[slot],
+            recv_sem=recv_sems.at[far], device_id=(place[0] + one, place[1] + two),
+            device_id_type=pl.DeviceIdType.MESH,
+        )
+        pl.when(present[slot])(copy.start)
+        copies.append(copy)
+
     fill_up(up_ref, table_ref)
+    band_ref[...] = jnp.zeros(band_ref.shape, band_ref.dtype)
+    fill_band(first_ref, band_ref)
+
+    for slot, (one, two) in enumerate(DIRECTIONS):
+        incoming = pltpu.make_async_remote_copy(
+            src_ref=own_ref, dst_ref=staging_ref.at[slot], send_sem=send_sems.at[slot],
+            recv_sem=recv_sems.at[slot], device_id=(place[0] + one, place[1] + two),
+            device_id_type=pl.DeviceIdType.MESH,
+        )
+
+        @pl.when(present[slot])
+        def _():
+            copies[slot].wait_send()
+            incoming.wait_recv()
+
+    size_one = own_ref.shape[0]
+    ext = halo_rows(own_ref, staging_ref, size_one)
     groups = 4
-    rows_in = shifts_ref.shape[1] // groups
+    channels = table_ref.shape[1] // groups
+    lane = lax.broadcasted_iota(jnp.int32, ((size_one + 1) * own_ref.shape[1], 128), 1)
+    windows = []
+    for high_one in (0, 1):
+        for high_two in (0, 1):
+            shifted_rows = [
+                ext[m + 1 - high_one] if high_two else pltpu.roll(ext[m + 1 - high_one], own_ref.shape[1] - 1, 0)
+                for m in range(size_one + 1)
+            ]
+            rows = jnp.concatenate(shifted_rows, axis=0)
+            parts = []
+            for g in range(groups):
+                rolled = pltpu.roll(rows, (channels - channels * g) % 128, 1)
+                keep = lane < 3 * channels
+                if g == 0:
+                    keep = keep & (lane >= channels)
+                if g == groups - 1:
+                    keep = keep & (lane < 2 * channels)
+                parts.append(jnp.where(keep, rolled, 0.0))
+            windows.append(jnp.concatenate(parts, axis=0).astype(jnp.bfloat16))
+    rows_in = (size_one + 1) * own_ref.shape[1]
     phases = []
     for phase_one in range(4):
         for phase_two in range(4):
@@ -126,7 +205,7 @@
                 for high_two in (0, 1):
                     taps = (4 * high_one + phase_one) * 8 + 4 * high_two + phase_two
                     term = jnp.dot(
-                        shifts_ref[high_one * 2 + high_two], table_ref[taps],
+                        windows[high_one * 2 + high_two], table_ref[taps],
                         preferred_element_type=jnp.float32,
                     )
                     total = term if total is None else total + term
@@ -136,8 +215,6 @@
     phase_rows = silu(jnp.concatenate(phases, axis=0)).astype(jnp.bfloat16)
     base = jnp.dot(pick_ref[...], phase_rows, preferred_element_type=jnp.float32)
     base = jnp.where(base_keep_ref[...] > 0, base, 0.0)
-    band_ref[...] = jnp.zeros(band_ref.shape, band_ref.dtype)
-    fill_band(first_ref, band_ref)
     hidden_count = (rows_out + 2) * width
     first = conv_rows(shifted(base), band_ref, width, hidden_count)
     hidden = jnp.where(hidden_keep_ref[...] > 0, silu(first), 0.0)
@@ -164,21 +241,7 @@
     own_rows, own_cols = 4 * size_one, 4 * size_two
     lanes = 4 * coarse_depth * channels
     width, span = 32, 8
-    coarse_ext = extended_2(coarse_field, (("strike", 0), ("dip", 1)), 1)
-    shifts = jnp.stack(
-        [
-            jnp.pad(
-                coarse_ext[1 - one : size_one + 2 - one, 1 - two : size_two + 2 - two],
-                ((0, 0), (0, span - size_two - 1), (0, 0)),
-            )
-            for one in (0, 1)
-            for two in (0, 1)
-        ]
-    ).reshape(4, (size_one + 1) * span, -1)
-    shifts = jnp.pad(shifts, ((0, 0), (0, 0), (channels, channels)))
-    shifts = jnp.stack(
-        [shifts[:, :, channels * g : channels * (g + 3)] for g in range(coarse_depth)], axis=1
-    ).reshape(4, coarse_depth * (size_one + 1) * span, 3 * channels)
+    own = jnp.pad(coarse_field.astype(jnp.float32), ((0, 0), (0, span - size_two), (0, 0)))
     rows_all = inside("strike", own_rows + 4, own_rows, 2)
     cols_all = inside("dip", own_cols + 4, own_cols, 2)
     cols_all = jnp.pad(cols_all, (0, width - own_cols - 4))
@@ -188,17 +251,22 @@
     hidden_keep = rows_all[1 : own_rows + 3, None] & cols_hidden[None, :]
     hidden_keep = hidden_keep.astype(jnp.float32).reshape(-1, 1)
     vmem = pl.BlockSpec(memory_space=pltpu.VMEM)
+    grid_shape = (lax.axis_size("strike"), lax.axis_size("dip"))
     return pl.pallas_call(
-        lambda *refs: block_kernel(width, own_rows, own_cols, *refs),
+        lambda *refs: block_kernel(width, own_rows, own_cols, grid_shape, *refs),
         out_shape=jax.ShapeDtypeStruct((own_rows, own_cols, lanes), jnp.bfloat16),
         in_specs=[vmem] * 7,
         out_specs=vmem,
         scratch_shapes=[
             pltpu.VMEM((9, lanes, lanes), jnp.bfloat16),
-            pltpu.VMEM((64, 3 * channels, 128), jnp.bfloat16),
+            pltpu.VMEM((64, 4 * channels, 128), jnp.bfloat16),
+            pltpu.VMEM((len(DIRECTIONS),) + own.shape, jnp.float32),
+            pltpu.SemaphoreType.DMA((len(DIRECTIONS),)),
+            pltpu.SemaphoreType.DMA((len(DIRECTIONS),)),
         ],
+        compiler_params=pltpu.CompilerParams(collective_id=0, has_side_effects=True),
     )(
-        shifts,
+        own,
         up_weight.reshape(-1, channels),
         picker(own_rows + 4, own_cols + 4, width, span),
         base_keep,

time: 41 us -> 27.7 us (0.68)
  the two profiles are of different devices: /device:TPU:193 before, /device:TPU:129 now
where the time goes in v6:
time: 27.7 us; the launch traced here: 27.5 us
  Pallas kernels  21 us (76%)
  local copies, waits for them, and re-layouts  3.83 us (14%)
  other arithmetic  2.71 us (10%)
    pallas_call x1, Pallas kernels, body(): pl.pallas_call(lambda *refs: block_kernel(width, own_rows, own_cols, grid...  21 us
    unnamed x1, local copies, waits for them, and re-layouts  1.67 us
    pad x1, other arithmetic, body(): jnp.pad(coarse_field.astype(jnp.float32), ((0, 0), (0, span - size_two),...  1.3 us
    convert_element_type x1, other arithmetic, picker(): return chosen.astype(jnp.bfloat16)  1.22 us
    convert_element_type x1, local copies, waits for them, and re-layouts, body(): (rows_all[:, None] & cols_all[None, :]).astype(jnp.float32).reshape(-1, 1)  1.06 us
    convert_element_type x1, local copies, waits for them, and re-layouts, body(): hidden_keep = hidden_keep.astype(jnp.float32).reshape(-1, 1)  1.02 us

profile of v6, /device:TPU:129, one launch (start us, length us, event | category | flops | bytes accessed | tf_op | source)
XLA Modules:
  0.0 27.5 jit_solution(18289678429907936048)
XLA Ops:
  0.0 0.1 slice.3
  0.1 0.1 and_convert_fusion
  0.2 0.1 and_convert_fusion.1
  0.3 1.3 %pad_convert_fusion.refs_0_ = f32[4,8,128]{2,1,0:T(8,128)} fusion(bf16[4,4,128]{2,1,0:T(4,128)(2,1)} %param.4), kind=kLoop, calls=%fused_computation.12 | loop fusion | flops 4096 | bytes 20480 | tf_op jit(solution)/shard_map/jit(_pad)/pad | solution.py:244
  1.6 1.0 %reshape.164.refs_4_ = f32[576,1]{1,0:T(8,128)} reshape(f32[18,32]{1,0:T(8,128)S(1)} %and_convert_fusion) | data formatting | bytes 4608 | tf_op jit(solution)/shard_map/convert_element_type | solution.py:252
  2.6 1.1 %reshape.163.refs_3_ = f32[640,1]{1,0:T(8,128)} reshape(f32[20,32]{1,0:T(8,128)S(1)} %and_convert_fusion.1) | data formatting | bytes 5120 | tf_op jit(solution)/shard_map/convert_element_type | solution.py:248
  3.7 1.2 %fusion.1.refs_2_ = bf16[640,640]{1,0:T(8,128)(2,1)} fusion(s32[640]{0:T(1024)S(1)} %fusion.12, pred[640]{0:T(1024)(128)(4,1)S(1)} %fusion.15), kind=kLoop, calls=%fused_computation.2 | loop fusion | flops 1228800 | bytes 822400 | tf_op jit(solution)/shard_map/convert_element_type | solution.py:234
  4.9 21.0 %shard_map.46 = bf16[16,16,512]{2,1,0:T(8,128)(2,1)} custom-call(f32[4,8,128]{2,1,0:T(8,128)} %pad_convert_fusion.refs_0_, bf16[16384,32]{1,0:T(8,128)(2,1)} %bitcast.3, bf16[640,640]{1,0:T(8,128)(2,1)} %fusion.1.refs_2_, f32[640,1]{1,0:T(8,128)} %reshape.163.refs_3_, f32[576,1]{1,0:T(8,128)} %reshape.164.refs_4_, bf16[864,32]{1,0:T(8,128)(2,1)} %bitcast.4, ...), custom_call_target="tpu_custom_call" | custom-call | tf_op jit(solution)/shard_map/pallas_call | solution.py:255
  25.9 1.7 %copy.8 = bf16[16,16,512]{2,1,0:T(8,128)(2,1)} copy(bf16[16,16,512]{2,1,0:T(8,128)(2,1)} %shard_map.46) | data formatting | bytes 524288
  (5 shorter events, 0.0 us)

commit v7 on v6

--- a/solution.py
+++ b/solution.py
@@ -1,5 +1,6 @@
 import jax
 import jax.numpy as jnp
+import ml_dtypes
 import numpy as np
 from jax import lax
 from jax.experimental import pallas as pl
@@ -7,12 +8,6 @@
 from jax.sharding import PartitionSpec as P
 
 HIGHEST = lax.Precision.HIGHEST
-
-
-def inside(axis, count, own, halo):
-    place = lax.axis_index(axis)
-    local = jnp.arange(count) - halo
-    return ((local >= 0) | (place > 0)) & ((local < own) | (place < lax.axis_size(axis) - 1))
 
 
 def fill_band(weight_ref, band_ref):
@@ -48,13 +43,30 @@
 
 
 def conv_rows(parts, band_ref, width, count):
-    total = None
-    for one in range(3):
-        for two in range(3):
-            window = parts[two][one * width : one * width + count]
-            term = jnp.dot(window, band_ref[one * 3 + two], preferred_element_type=jnp.float32)
-            total = term if total is None else total + term
-    return total
+    lanes = band_ref.shape[1]
+    halves = []
+    for half in range(lanes // 256):
+        low = min(max(256 * half - 128, 0), lanes - 384)
+        total = None
+        for one in range(3):
+            for two in range(3):
+                window = parts[two][one * width : one * width + count, low : low + 384]
+                term = jnp.dot(
+                    window, band_ref[one * 3 + two, low : low + 384, 256 * half : 256 * half + 256],
+                    preferred_element_type=jnp.float32,
+                )
+                total = term if total is None else total + term
+        halves.append(total)
+    return jnp.concatenate(halves, axis=1)
+
+
+def keep_rows(place, grid_shape, own, first, count, width, low, high):
+    index = lax.broadcasted_iota(jnp.int32, (count * width, 1), 0)
+    one = lax.shift_right_logical(index, 5) + first - 2
+    two = jnp.bitwise_and(index, 31) - 2
+    keep = ((one >= 0) | (place[0] > 0)) & ((one < own[0]) | (place[0] < grid_shape[0] - 1))
+    keep = keep & ((two >= 0) | (place[1] > 0)) & ((two < own[1]) | (place[1] < grid_shape[1] - 1))
+    return keep & (two + 2 >= low) & (two + 2 < high)
 
 
 def silu(values):
@@ -122,7 +134,7 @@
 
 def block_kernel(
     width, rows_out, cols_out, grid_shape,
-    own_ref, up_ref, pick_ref, base_keep_ref, hidden_keep_ref, first_ref, second_ref,
+    own_ref, up_ref, pick_ref, first_ref, second_ref,
     out_ref, band_ref, table_ref, staging_ref, send_sems, recv_sems,
 ):
     place = (lax.axis_index("strike"), lax.axis_index("dip"))
@@ -214,10 +226,12 @@
             )
     phase_rows = silu(jnp.concatenate(phases, axis=0)).astype(jnp.bfloat16)
     base = jnp.dot(pick_ref[...], phase_rows, preferred_element_type=jnp.float32)
-    base = jnp.where(base_keep_ref[...] > 0, base, 0.0)
+    own = (rows_out, cols_out)
+    base = jnp.where(keep_rows(place, grid_shape, own, 0, rows_out + 4, width, 0, cols_out + 4), base, 0.0)
     hidden_count = (rows_out + 2) * width
     first = conv_rows(shifted(base), band_ref, width, hidden_count)
-    hidden = jnp.where(hidden_keep_ref[...] > 0, silu(first), 0.0)
+    hidden_keep = keep_rows(place, grid_shape, own, 1, rows_out + 2, width, 1, cols_out + 3)
+    hidden = jnp.where(hidden_keep, silu(first), 0.0)
     fill_band(second_ref, band_ref)
     out_count = rows_out * width
     second = conv_rows(shifted(hidden), band_ref, width, out_count)
@@ -227,11 +241,11 @@
 
 
 def picker(rows, cols, width, span):
-    place = jnp.arange(rows * width)
+    place = np.arange(rows * width)
     one, two = place // width, place % width
     source = ((one % 4) * 4 + two % 4) * (rows // 4) * span + (one // 4) * span + two // 4
-    chosen = (jnp.arange(rows * width)[None, :] == source[:, None]) & (two < cols)[:, None]
-    return chosen.astype(jnp.bfloat16)
+    chosen = (np.arange(16 * (rows // 4) * span)[None, :] == source[:, None]) & (two < cols)[:, None]
+    return chosen.astype(ml_dtypes.bfloat16)
 
 
 def body(coarse_field, up_weight, first_weight, second_weight):
@@ -242,20 +256,12 @@
     lanes = 4 * coarse_depth * channels
     width, span = 32, 8
     own = jnp.pad(coarse_field.astype(jnp.float32), ((0, 0), (0, span - size_two), (0, 0)))
-    rows_all = inside("strike", own_rows + 4, own_rows, 2)
-    cols_all = inside("dip", own_cols + 4, own_cols, 2)
-    cols_all = jnp.pad(cols_all, (0, width - own_cols - 4))
-    base_keep = (rows_all[:, None] & cols_all[None, :]).astype(jnp.float32).reshape(-1, 1)
-    position = jnp.arange(width)
-    cols_hidden = cols_all & (position >= 1) & (position < own_cols + 3)
-    hidden_keep = rows_all[1 : own_rows + 3, None] & cols_hidden[None, :]
-    hidden_keep = hidden_keep.astype(jnp.float32).reshape(-1, 1)
     vmem = pl.BlockSpec(memory_space=pltpu.VMEM)
     grid_shape = (lax.axis_size("strike"), lax.axis_size("dip"))
     return pl.pallas_call(
         lambda *refs: block_kernel(width, own_rows, own_cols, grid_shape, *refs),
         out_shape=jax.ShapeDtypeStruct((own_rows, own_cols, lanes), jnp.bfloat16),
-        in_specs=[vmem] * 7,
+        in_specs=[vmem] * 5,
         out_specs=vmem,
         scratch_shapes=[
             pltpu.VMEM((9, lanes, lanes), jnp.bfloat16),
@@ -268,9 +274,7 @@
     )(
         own,
         up_weight.reshape(-1, channels),
-        picker(own_rows + 4, own_cols + 4, width, span),
-        base_keep,
-        hidden_keep,
+        jnp.asarray(picker(own_rows + 4, own_cols + 4, width, span)),
         first_weight.reshape(-1, channels),
         second_weight.reshape(-1, channels),
     )

time: 27.7 us -> 23.8 us (0.86)
  local copies, waits for them, and re-layouts: 3.83 us -> 1.67 us
  other arithmetic: 2.71 us -> 1.29 us
  Pallas kernels: 21 us -> 20.7 us
    convert_element_type x2 -> x0, local copies, waits for them, and re-layouts: 2.09 us -> none  [the longest x1 1.06 us: body(): (rows_all[:, None] & cols_all[None, :]).astype(jnp.float32).reshape(-1, 1)]
    convert_element_type x3 -> x0, other arithmetic: 1.37 us -> none  [the longest x1 1.22 us: picker(): return chosen.astype(jnp.bfloat16)]
    pallas_call x1, Pallas kernels: 21 us -> 20.7 us  [body(): pl.pallas_call(lambda *refs: block_kernel(width, own_rows, own_cols, grid...]
where the time goes in v7:
time: 23.8 us; the launch traced here: 23.7 us
  Pallas kernels  20.7 us (87%)
  local copies, waits for them, and re-layouts  1.67 us (7%)
  other arithmetic  1.29 us (5%)
    pallas_call x1, Pallas kernels, body(): pl.pallas_call(lambda *refs: block_kernel(width, own_rows, own_cols, grid...  20.7 us
    unnamed x1, local copies, waits for them, and re-layouts  1.67 us
    pad x1, other arithmetic, body(): jnp.pad(coarse_field.astype(jnp.float32), ((0, 0), (0, span - size_two),...  1.29 us

profile of v7, /device:TPU:129, one launch (start us, length us, event | category | flops | bytes accessed | tf_op | source)
XLA Modules:
  0.0 23.7 jit_solution(48279609821592131)
XLA Ops:
  0.0 1.3 %pad_convert_fusion.refs_0_ = f32[4,8,128]{2,1,0:T(8,128)} fusion(bf16[4,4,128]{2,1,0:T(4,128)(2,1)} %param.5), kind=kLoop, calls=%fused_computation | loop fusion | flops 4096 | bytes 20480 | tf_op jit(solution)/shard_map/jit(_pad)/pad | solution.py:258
  1.3 20.7 %shard_map.55 = bf16[16,16,512]{2,1,0:T(8,128)(2,1)} custom-call(f32[4,8,128]{2,1,0:T(8,128)} %pad_convert_fusion.refs_0_, bf16[16384,32]{1,0:T(8,128)(2,1)} %bitcast.3, bf16[640,640]{1,0:T(8,128)(2,1)} %constant.6.clone.refs_2_, bf16[864,32]{1,0:T(8,128)(2,1)} %bitcast.4, bf16[864,32]{1,0:T(8,128)(2,1)} %bitcast.5), custom_call_target="tpu_custom_call" | custom-call | tf_op jit(solution)/shard_map/pallas_call | solution.py:261
  22.0 1.7 %copy.7 = bf16[16,16,512]{2,1,0:T(8,128)(2,1)} copy(bf16[16,16,512]{2,1,0:T(8,128)(2,1)} %shard_map.55) | data formatting | bytes 524288

commit v8 on v7

--- a/solution.py
+++ b/solution.py
@@ -111,13 +111,16 @@
 DIRECTIONS = [(-1, -1), (-1, 0), (-1, 1), (0, -1), (0, 1), (1, -1), (1, 0), (1, 1)]
 
 
-def halo_rows(own_ref, staging_ref, size_one):
-    sub = lax.broadcasted_iota(jnp.int32, own_ref.shape[1:], 0)
+def halo_rows(own_ref, staging_ref, size_one, span):
+    sub = lax.broadcasted_iota(jnp.int32, (span, own_ref.shape[2]), 0)
 
     def block_row(one, two, row):
         if (one, two) == (0, 0):
-            return own_ref[row]
-        return staging_ref[DIRECTIONS.index((one, two)), row]
+            values = own_ref[row]
+        else:
+            values = staging_ref[DIRECTIONS.index((one, two)), row]
+        values = values.astype(jnp.float32)
+        return jnp.concatenate([values, jnp.zeros((span - values.shape[0], values.shape[1]), jnp.float32)], axis=0)
 
     rows = []
     for ext in range(size_one + 2):
@@ -186,15 +189,16 @@
             incoming.wait_recv()
 
     size_one = own_ref.shape[0]
-    ext = halo_rows(own_ref, staging_ref, size_one)
+    span = 8
+    ext = halo_rows(own_ref, staging_ref, size_one, span)
     groups = 4
     channels = table_ref.shape[1] // groups
-    lane = lax.broadcasted_iota(jnp.int32, ((size_one + 1) * own_ref.shape[1], 128), 1)
+    lane = lax.broadcasted_iota(jnp.int32, ((size_one + 1) * span, 128), 1)
     windows = []
     for high_one in (0, 1):
         for high_two in (0, 1):
             shifted_rows = [
-                ext[m + 1 - high_one] if high_two else pltpu.roll(ext[m + 1 - high_one], own_ref.shape[1] - 1, 0)
+                ext[m + 1 - high_one] if high_two else pltpu.roll(ext[m + 1 - high_one], span - 1, 0)
                 for m in range(size_one + 1)
             ]
             rows = jnp.concatenate(shifted_rows, axis=0)
@@ -208,7 +212,7 @@
                     keep = keep & (lane < 2 * channels)
                 parts.append(jnp.where(keep, rolled, 0.0))
             windows.append(jnp.concatenate(parts, axis=0).astype(jnp.bfloat16))
-    rows_in = (size_one + 1) * own_ref.shape[1]
+    rows_in = (size_one + 1) * span
     phases = []
     for phase_one in range(4):
         for phase_two in range(4):
@@ -255,7 +259,6 @@
     own_rows, own_cols = 4 * size_one, 4 * size_two
     lanes = 4 * coarse_depth * channels
     width, span = 32, 8
-    own = jnp.pad(coarse_field.astype(jnp.float32), ((0, 0), (0, span - size_two), (0, 0)))
     vmem = pl.BlockSpec(memory_space=pltpu.VMEM)
     grid_shape = (lax.axis_size("strike"), lax.axis_size("dip"))
     return pl.pallas_call(
@@ -266,13 +269,13 @@
         scratch_shapes=[
             pltpu.VMEM((9, lanes, lanes), jnp.bfloat16),
             pltpu.VMEM((64, 4 * channels, 128), jnp.bfloat16),
-            pltpu.VMEM((len(DIRECTIONS),) + own.shape, jnp.float32),
+            pltpu.VMEM((len(DIRECTIONS),) + coarse_field.shape, coarse_field.dtype),
             pltpu.SemaphoreType.DMA((len(DIRECTIONS),)),
             pltpu.SemaphoreType.DMA((len(DIRECTIONS),)),
         ],
         compiler_params=pltpu.CompilerParams(collective_id=0, has_side_effects=True),
     )(
-        own,
+        coarse_field,
         up_weight.reshape(-1, channels),
         jnp.asarray(picker(own_rows + 4, own_cols + 4, width, span)),
         first_weight.reshape(-1, channels),

time: 23.8 us -> 22.3 us (0.937)
  other arithmetic: 1.29 us -> 0 us
    pad x1 -> x0, other arithmetic: 1.29 us -> none  [body(): jnp.pad(coarse_field.astype(jnp.float32), ((0, 0), (0, span - size_two),...]
where the time goes in v8:
time: 22.3 us; the launch traced here: 22.2 us
  Pallas kernels  20.6 us (92%)
  local copies, waits for them, and re-layouts  1.67 us (7%)
    pallas_call x1, Pallas kernels, body(): pl.pallas_call(lambda *refs: block_kernel(width, own_rows, own_cols, grid...  20.6 us
    unnamed x1, local copies, waits for them, and re-layouts  1.67 us

profile of v8, /device:TPU:129, one launch (start us, length us, event | category | flops | bytes accessed | tf_op | source)
XLA Modules:
  0.0 22.2 jit_solution(1602516195327391820)
XLA Ops:
  0.0 20.6 %shard_map.55 = bf16[16,16,512]{2,1,0:T(8,128)(2,1)} custom-call(bf16[4,4,128]{2,1,0:T(4,128)(2,1)} %refs_0_.1, bf16[16384,32]{1,0:T(8,128)(2,1)} %bitcast.3, bf16[640,640]{1,0:T(8,128)(2,1)} %constant.2.clone.refs_2_, bf16[864,32]{1,0:T(8,128)(2,1)} %bitcast.4, bf16[864,32]{1,0:T(8,128)(2,1)} %bitcast.5), custom_call_target="tpu_custom_call" | custom-call | tf_op jit(solution)/shard_map/pallas_call | solution.py:264
  20.6 1.7 %copy.7 = bf16[16,16,512]{2,1,0:T(8,128)(2,1)} copy(bf16[16,16,512]{2,1,0:T(8,128)(2,1)} %shard_map.55) | data formatting | bytes 524288

commit v9 on v8

--- a/solution.py
+++ b/solution.py
@@ -158,6 +158,7 @@
                 barrier, 1, device_id=(place[0] + one, place[1] + two),
                 device_id_type=pl.DeviceIdType.MESH,
             )
+    fill_up(up_ref, table_ref)
     count = sum(p.astype(jnp.int32) for p in present)
     pl.semaphore_wait(barrier, count)
 
@@ -172,7 +173,6 @@
         pl.when(present[slot])(copy.start)
         copies.append(copy)
 
-    fill_up(up_ref, table_ref)
     band_ref[...] = jnp.zeros(band_ref.shape, band_ref.dtype)
     fill_band(first_ref, band_ref)
 

time: 22.3 us -> 22.3 us (level)
  the two profiles are of different devices: /device:TPU:129 before, /device:TPU:193 now
where the time goes in v9:
time: 22.3 us; the launch traced here: 22.1 us
  Pallas kernels  20.4 us (91%)
  local copies, waits for them, and re-layouts  1.67 us (7%)
    pallas_call x1, Pallas kernels, body(): pl.pallas_call(lambda *refs: block_kernel(width, own_rows, own_cols, grid...  20.4 us
    unnamed x1, local copies, waits for them, and re-layouts  1.67 us

profile of v9, /device:TPU:193, one launch (start us, length us, event | category | flops | bytes accessed | tf_op | source)
XLA Modules:
  0.0 22.1 jit_solution(10876764664569295509)
XLA Ops:
  0.0 20.4 %shard_map.55 = bf16[16,16,512]{2,1,0:T(8,128)(2,1)} custom-call(bf16[4,4,128]{2,1,0:T(4,128)(2,1)} %refs_0_.1, bf16[16384,32]{1,0:T(8,128)(2,1)} %bitcast.3, bf16[640,640]{1,0:T(8,128)(2,1)} %constant.2.clone.refs_2_, bf16[864,32]{1,0:T(8,128)(2,1)} %bitcast.4, bf16[864,32]{1,0:T(8,128)(2,1)} %bitcast.5), custom_call_target="tpu_custom_call" | custom-call | tf_op jit(solution)/shard_map/pallas_call | solution.py:264
  20.4 1.7 %copy.7 = bf16[16,16,512]{2,1,0:T(8,128)(2,1)} copy(bf16[16,16,512]{2,1,0:T(8,128)(2,1)} %shard_map.55) | data formatting | bytes 524288

commit v10 on v9

--- a/solution.py
+++ b/solution.py
@@ -73,7 +73,7 @@
     return values / (1.0 + jnp.exp(-values))
 
 
-def fill_up(weight_ref, table_ref):
+def fill_up(weight_ref, table_ref, source_ref=None, copy_sems=None):
     channels = weight_ref.shape[1]
     lane = lax.broadcasted_iota(jnp.int32, (channels, 128), 1)
     spread_out = (lane % channels == lax.broadcasted_iota(jnp.int32, (channels, 128), 0))
@@ -86,6 +86,11 @@
 
     def one(step, carry):
         start = pl.multiple_of(step * chunk * span, chunk * span)
+        if source_ref is not None:
+            pltpu.make_async_copy(
+                source_ref.at[pl.ds(start, chunk * span)], weight_ref.at[pl.ds(start, chunk * span)],
+                copy_sems.at[step],
+            ).wait()
         tiled = jnp.dot(
             weight_ref[pl.ds(start, chunk * span)], spread_out, preferred_element_type=jnp.float32
         )
@@ -138,8 +143,14 @@
 def block_kernel(
     width, rows_out, cols_out, grid_shape,
     own_ref, up_ref, pick_ref, first_ref, second_ref,
-    out_ref, band_ref, table_ref, staging_ref, send_sems, recv_sems,
+    out_ref, band_ref, table_ref, staging_ref, send_sems, recv_sems, up_vmem, up_sems,
 ):
+    pieces = up_sems.shape[0]
+    piece = up_vmem.shape[0] // pieces
+    for step in range(pieces):
+        pltpu.make_async_copy(
+            up_ref.at[pl.ds(step * piece, piece)], up_vmem.at[pl.ds(step * piece, piece)], up_sems.at[step]
+        ).start()
     place = (lax.axis_index("strike"), lax.axis_index("dip"))
     present = [
         (place[0] + one >= 0) & (place[0] + one < grid_shape[0]) & (place[1] + two >= 0) & (place[1] + two < grid_shape[1])
@@ -158,7 +169,8 @@
                 barrier, 1, device_id=(place[0] + one, place[1] + two),
                 device_id_type=pl.DeviceIdType.MESH,
             )
-    fill_up(up_ref, table_ref)
+    band_ref[...] = jnp.zeros(band_ref.shape, band_ref.dtype)
+    fill_up(up_vmem, table_ref, up_ref, up_sems)
     count = sum(p.astype(jnp.int32) for p in present)
     pl.semaphore_wait(barrier, count)
 
@@ -173,7 +185,6 @@
         pl.when(present[slot])(copy.start)
         copies.append(copy)
 
-    band_ref[...] = jnp.zeros(band_ref.shape, band_ref.dtype)
     fill_band(first_ref, band_ref)
 
     for slot, (one, two) in enumerate(DIRECTIONS):
@@ -264,7 +275,7 @@
     return pl.pallas_call(
         lambda *refs: block_kernel(width, own_rows, own_cols, grid_shape, *refs),
         out_shape=jax.ShapeDtypeStruct((own_rows, own_cols, lanes), jnp.bfloat16),
-        in_specs=[vmem] * 5,
+        in_specs=[vmem, pl.BlockSpec(memory_space=pl.ANY)] + [vmem] * 3,
         out_specs=vmem,
         scratch_shapes=[
             pltpu.VMEM((9, lanes, lanes), jnp.bfloat16),
@@ -272,6 +283,8 @@
             pltpu.VMEM((len(DIRECTIONS),) + coarse_field.shape, coarse_field.dtype),
             pltpu.SemaphoreType.DMA((len(DIRECTIONS),)),
             pltpu.SemaphoreType.DMA((len(DIRECTIONS),)),
+            pltpu.VMEM((up_weight.size // channels, channels), up_weight.dtype),
+            pltpu.SemaphoreType.DMA((8,)),
         ],
         compiler_params=pltpu.CompilerParams(collective_id=0, has_side_effects=True),
     )(

time: 22.3 us -> 22.1 us (level)
  no operation moved by 1% of the time
where the time goes in v10:
time: 22.1 us; the launch traced here: 22 us
  Pallas kernels  20.3 us (92%)
  local copies, waits for them, and re-layouts  1.67 us (8%)
    pallas_call x1, Pallas kernels, body(): pl.pallas_call(lambda *refs: block_kernel(width, own_rows, own_cols, grid...  20.3 us
    unnamed x1, local copies, waits for them, and re-layouts  1.67 us

profile of v10, /device:TPU:193, one launch (start us, length us, event | category | flops | bytes accessed | tf_op | source)
XLA Modules:
  0.0 22.0 jit_solution(10405641847312432588)
XLA Ops:
  0.0 20.3 %shard_map.55 = bf16[16,16,512]{2,1,0:T(8,128)(2,1)} custom-call(bf16[4,4,128]{2,1,0:T(4,128)(2,1)} %refs_0_.1, bf16[16384,32]{1,0:T(8,128)(2,1)} %bitcast.3, bf16[640,640]{1,0:T(8,128)(2,1)} %constant.2.clone.refs_2_, bf16[864,32]{1,0:T(8,128)(2,1)} %bitcast.4, bf16[864,32]{1,0:T(8,128)(2,1)} %bitcast.5), custom_call_target="tpu_custom_call" | custom-call | tf_op jit(solution)/shard_map/pallas_call | solution.py:275
  20.3 1.7 %copy.7 = bf16[16,16,512]{2,1,0:T(8,128)(2,1)} copy(bf16[16,16,512]{2,1,0:T(8,128)(2,1)} %shard_map.55) | data formatting | bytes 524288

commit v11 on v10

--- a/solution.py
+++ b/solution.py
@@ -82,7 +82,7 @@
     per_group = 128 // channels
     span = 8 * channels
 
-    chunk = 8
+    chunk = 64
 
     def one(step, carry):
         start = pl.multiple_of(step * chunk * span, chunk * span)
@@ -284,7 +284,7 @@
             pltpu.SemaphoreType.DMA((len(DIRECTIONS),)),
             pltpu.SemaphoreType.DMA((len(DIRECTIONS),)),
             pltpu.VMEM((up_weight.size // channels, channels), up_weight.dtype),
-            pltpu.SemaphoreType.DMA((8,)),
+            pltpu.SemaphoreType.DMA((1,)),
         ],
         compiler_params=pltpu.CompilerParams(collective_id=0, has_side_effects=True),
     )(

time: 22.1 us -> 24.4 us (1.10)
  Pallas kernels: 20.3 us -> 22.5 us
    pallas_call x1, Pallas kernels: 20.3 us -> 22.5 us  [body(): pl.pallas_call(lambda *refs: block_kernel(width, own_rows, own_cols, grid...]
where the time goes in v11:
time: 24.4 us; the launch traced here: 24.2 us
  Pallas kernels  22.5 us (92%)
  local copies, waits for them, and re-layouts  1.67 us (7%)
    pallas_call x1, Pallas kernels, body(): pl.pallas_call(lambda *refs: block_kernel(width, own_rows, own_cols, grid...  22.5 us
    unnamed x1, local copies, waits for them, and re-layouts  1.67 us

profile of v11, /device:TPU:193, one launch (start us, length us, event | category | flops | bytes accessed | tf_op | source)
XLA Modules:
  0.0 24.2 jit_solution(14519244476753634834)
XLA Ops:
  0.0 22.5 %shard_map.55 = bf16[16,16,512]{2,1,0:T(8,128)(2,1)} custom-call(bf16[4,4,128]{2,1,0:T(4,128)(2,1)} %refs_0_.1, bf16[16384,32]{1,0:T(8,128)(2,1)} %bitcast.3, bf16[640,640]{1,0:T(8,128)(2,1)} %constant.2.clone.refs_2_, bf16[864,32]{1,0:T(8,128)(2,1)} %bitcast.4, bf16[864,32]{1,0:T(8,128)(2,1)} %bitcast.5), custom_call_target="tpu_custom_call" | custom-call | tf_op jit(solution)/shard_map/pallas_call | solution.py:275
  22.5 1.7 %copy.7 = bf16[16,16,512]{2,1,0:T(8,128)(2,1)} copy(bf16[16,16,512]{2,1,0:T(8,128)(2,1)} %shard_map.55) | data formatting | bytes 524288

commit v12 on v11

--- a/solution.py
+++ b/solution.py
@@ -82,7 +82,7 @@
     per_group = 128 // channels
     span = 8 * channels
 
-    chunk = 64
+    chunk = 16
 
     def one(step, carry):
         start = pl.multiple_of(step * chunk * span, chunk * span)
@@ -284,7 +284,7 @@
             pltpu.SemaphoreType.DMA((len(DIRECTIONS),)),
             pltpu.SemaphoreType.DMA((len(DIRECTIONS),)),
             pltpu.VMEM((up_weight.size // channels, channels), up_weight.dtype),
-            pltpu.SemaphoreType.DMA((1,)),
+            pltpu.SemaphoreType.DMA((4,)),
         ],
         compiler_params=pltpu.CompilerParams(collective_id=0, has_side_effects=True),
     )(

time: 24.4 us -> 21.8 us (0.89)
  Pallas kernels: 22.5 us -> 19.9 us
    pallas_call x1, Pallas kernels: 22.5 us -> 19.9 us  [body(): pl.pallas_call(lambda *refs: block_kernel(width, own_rows, own_cols, grid...]
where the time goes in v12:
time: 21.8 us; the launch traced here: 21.6 us
  Pallas kernels  19.9 us (91%)
  local copies, waits for them, and re-layouts  1.67 us (8%)
    pallas_call x1, Pallas kernels, body(): pl.pallas_call(lambda *refs: block_kernel(width, own_rows, own_cols, grid...  19.9 us
    unnamed x1, local copies, waits for them, and re-layouts  1.67 us

profile of v12, /device:TPU:193, one launch (start us, length us, event | category | flops | bytes accessed | tf_op | source)
XLA Modules:
  0.0 21.6 jit_solution(13271493556719076940)
XLA Ops:
  0.0 19.9 %shard_map.55 = bf16[16,16,512]{2,1,0:T(8,128)(2,1)} custom-call(bf16[4,4,128]{2,1,0:T(4,128)(2,1)} %refs_0_.1, bf16[16384,32]{1,0:T(8,128)(2,1)} %bitcast.3, bf16[640,640]{1,0:T(8,128)(2,1)} %constant.2.clone.refs_2_, bf16[864,32]{1,0:T(8,128)(2,1)} %bitcast.4, bf16[864,32]{1,0:T(8,128)(2,1)} %bitcast.5), custom_call_target="tpu_custom_call" | custom-call | tf_op jit(solution)/shard_map/pallas_call | solution.py:275
  20.0 1.7 %copy.7 = bf16[16,16,512]{2,1,0:T(8,128)(2,1)} copy(bf16[16,16,512]{2,1,0:T(8,128)(2,1)} %shard_map.55) | data formatting | bytes 524288

commit v13 on v12

--- a/solution.py
+++ b/solution.py
@@ -70,7 +70,7 @@
 
 
 def silu(values):
-    return values / (1.0 + jnp.exp(-values))
+    return 0.5 * values * (1.0 + jnp.tanh(0.5 * values))
 
 
 def fill_up(weight_ref, table_ref, source_ref=None, copy_sems=None):

time: 21.8 us -> 21.7 us (level)
  no operation moved by 1% of the time
where the time goes in v13:
time: 21.7 us; the launch traced here: 21.6 us
  Pallas kernels  19.9 us (92%)
  local copies, waits for them, and re-layouts  1.67 us (8%)
    pallas_call x1, Pallas kernels, body(): pl.pallas_call(lambda *refs: block_kernel(width, own_rows, own_cols, grid...  19.9 us
    unnamed x1, local copies, waits for them, and re-layouts  1.67 us

profile of v13, /device:TPU:193, one launch (start us, length us, event | category | flops | bytes accessed | tf_op | source)
XLA Modules:
  0.0 21.6 jit_solution(16707303235130089786)
XLA Ops:
  0.0 19.9 %shard_map.55 = bf16[16,16,512]{2,1,0:T(8,128)(2,1)} custom-call(bf16[4,4,128]{2,1,0:T(4,128)(2,1)} %refs_0_.1, bf16[16384,32]{1,0:T(8,128)(2,1)} %bitcast.3, bf16[640,640]{1,0:T(8,128)(2,1)} %constant.2.clone.refs_2_, bf16[864,32]{1,0:T(8,128)(2,1)} %bitcast.4, bf16[864,32]{1,0:T(8,128)(2,1)} %bitcast.5), custom_call_target="tpu_custom_call" | custom-call | tf_op jit(solution)/shard_map/pallas_call | solution.py:275
  19.9 1.7 %copy.7 = bf16[16,16,512]{2,1,0:T(8,128)(2,1)} copy(bf16[16,16,512]{2,1,0:T(8,128)(2,1)} %shard_map.55) | data formatting | bytes 524288

commit v14 on v13

--- a/solution.py
+++ b/solution.py
@@ -35,35 +35,31 @@
 
 def shifted(values):
     rows = values.shape[0]
-    return (
-        pltpu.roll(values, 1, 0).astype(jnp.bfloat16),
-        values.astype(jnp.bfloat16),
-        pltpu.roll(values, rows - 1, 0).astype(jnp.bfloat16),
-    )
+    return (pltpu.roll(values, 1, 0), values, pltpu.roll(values, rows - 1, 0))
 
 
 def conv_rows(parts, band_ref, width, count):
     lanes = band_ref.shape[1]
-    halves = []
-    for half in range(lanes // 256):
-        low = min(max(256 * half - 128, 0), lanes - 384)
-        total = None
-        for one in range(3):
-            for two in range(3):
-                window = parts[two][one * width : one * width + count, low : low + 384]
+    totals = [None] * (lanes // 256)
+    for one in range(3):
+        for two in range(3):
+            window = parts[two][one * width : one * width + count].astype(jnp.bfloat16)
+            for half in range(lanes // 256):
+                low = min(max(256 * half - 128, 0), lanes - 384)
                 term = jnp.dot(
-                    window, band_ref[one * 3 + two, low : low + 384, 256 * half : 256 * half + 256],
+                    window[:, low : low + 384],
+                    band_ref[one * 3 + two, low : low + 384, 256 * half : 256 * half + 256],
                     preferred_element_type=jnp.float32,
                 )
-                total = term if total is None else total + term
-        halves.append(total)
-    return jnp.concatenate(halves, axis=1)
+                totals[half] = term if totals[half] is None else totals[half] + term
+    return jnp.concatenate(totals, axis=1)
 
 
 def keep_rows(place, grid_shape, own, first, count, width, low, high):
     index = lax.broadcasted_iota(jnp.int32, (count * width, 1), 0)
-    one = lax.shift_right_logical(index, 5) + first - 2
-    two = jnp.bitwise_and(index, 31) - 2
+    whole = jnp.floor((index.astype(jnp.float32) + 0.5) / width).astype(jnp.int32)
+    one = whole + first - 2
+    two = index - whole * width - 2
     keep = ((one >= 0) | (place[0] > 0)) & ((one < own[0]) | (place[0] < grid_shape[0] - 1))
     keep = keep & ((two >= 0) | (place[1] > 0)) & ((two < own[1]) | (place[1] < grid_shape[1] - 1))
     return keep & (two + 2 >= low) & (two + 2 < high)
@@ -269,7 +265,7 @@
     size_one, size_two = coarse_field.shape[:2]
     own_rows, own_cols = 4 * size_one, 4 * size_two
     lanes = 4 * coarse_depth * channels
-    width, span = 32, 8
+    width, span = 24, 8
     vmem = pl.BlockSpec(memory_space=pltpu.VMEM)
     grid_shape = (lax.axis_size("strike"), lax.axis_size("dip"))
     return pl.pallas_call(

time: 21.7 us -> 20.5 us (0.945)
  Pallas kernels: 19.9 us -> 18.7 us
    pallas_call x1, Pallas kernels: 19.9 us -> 18.7 us  [body(): pl.pallas_call(lambda *refs: block_kernel(width, own_rows, own_cols, grid...]
where the time goes in v14:
time: 20.5 us; the launch traced here: 20.4 us
  Pallas kernels  18.7 us (91%)
  local copies, waits for them, and re-layouts  1.67 us (8%)
    pallas_call x1, Pallas kernels, body(): pl.pallas_call(lambda *refs: block_kernel(width, own_rows, own_cols, grid...  18.7 us
    unnamed x1, local copies, waits for them, and re-layouts  1.67 us

profile of v14, /device:TPU:193, one launch (start us, length us, event | category | flops | bytes accessed | tf_op | source)
XLA Modules:
  0.0 20.4 jit_solution(1965697371021633461)
XLA Ops:
  0.0 18.7 %shard_map.55 = bf16[16,16,512]{2,1,0:T(8,128)(2,1)} custom-call(bf16[4,4,128]{2,1,0:T(4,128)(2,1)} %refs_0_.1, bf16[16384,32]{1,0:T(8,128)(2,1)} %bitcast.3, bf16[480,640]{1,0:T(8,128)(2,1)} %constant.2.clone.refs_2_, bf16[864,32]{1,0:T(8,128)(2,1)} %bitcast.4, bf16[864,32]{1,0:T(8,128)(2,1)} %bitcast.5), custom_call_target="tpu_custom_call" | custom-call | tf_op jit(solution)/shard_map/pallas_call | solution.py:271
  18.7 1.7 %copy.7 = bf16[16,16,512]{2,1,0:T(8,128)(2,1)} copy(bf16[16,16,512]{2,1,0:T(8,128)(2,1)} %shard_map.55) | data formatting | bytes 524288

commit v15 on v14

--- a/solution.py
+++ b/solution.py
@@ -41,9 +41,13 @@
 def conv_rows(parts, band_ref, width, count):
     lanes = band_ref.shape[1]
     totals = [None] * (lanes // 256)
+    narrow = [part.astype(jnp.bfloat16) for part in parts]
     for one in range(3):
         for two in range(3):
-            window = parts[two][one * width : one * width + count].astype(jnp.bfloat16)
+            if (one * width) % 16 == 0:
+                window = narrow[two][one * width : one * width + count]
+            else:
+                window = parts[two][one * width : one * width + count].astype(jnp.bfloat16)
             for half in range(lanes // 256):
                 low = min(max(256 * half - 128, 0), lanes - 384)
                 term = jnp.dot(

time: 20.5 us -> 20.5 us (level)
  no operation moved by 1% of the time
where the time goes in v15:
time: 20.5 us; the launch traced here: 20.4 us
  Pallas kernels  18.7 us (91%)
  local copies, waits for them, and re-layouts  1.67 us (8%)
    pallas_call x1, Pallas kernels, body(): pl.pallas_call(lambda *refs: block_kernel(width, own_rows, own_cols, grid...  18.7 us
    unnamed x1, local copies, waits for them, and re-layouts  1.67 us

profile of v15, /device:TPU:193, one launch (start us, length us, event | category | flops | bytes accessed | tf_op | source)
XLA Modules:
  0.0 20.4 jit_solution(1287891035174874380)
XLA Ops:
  0.0 18.7 %shard_map.55 = bf16[16,16,512]{2,1,0:T(8,128)(2,1)} custom-call(bf16[4,4,128]{2,1,0:T(4,128)(2,1)} %refs_0_.1, bf16[16384,32]{1,0:T(8,128)(2,1)} %bitcast.3, bf16[480,640]{1,0:T(8,128)(2,1)} %constant.2.clone.refs_2_, bf16[864,32]{1,0:T(8,128)(2,1)} %bitcast.4, bf16[864,32]{1,0:T(8,128)(2,1)} %bitcast.5), custom_call_target="tpu_custom_call" | custom-call | tf_op jit(solution)/shard_map/pallas_call | solution.py:275
  18.7 1.7 %copy.7 = bf16[16,16,512]{2,1,0:T(8,128)(2,1)} copy(bf16[16,16,512]{2,1,0:T(8,128)(2,1)} %shard_map.55) | data formatting | bytes 524288

commit v16 on v14

--- a/solution.py
+++ b/solution.py
@@ -30,6 +30,19 @@
                         block = jnp.where(quarter == out_cell, tiled[row : row + channels], block)
                 band_ref[tap, pl.ds(cell * channels, channels), pl.ds(128 * group, 128)] = block.astype(
                     band_ref.dtype
+                )
+
+
+def zero_band(band_ref, channels):
+    cells = band_ref.shape[1] // channels
+    per_group = 128 // channels
+    for group in range(band_ref.shape[2] // 128):
+        low, high = (0, cells - per_group) if group < 2 else (per_group, cells)
+        written = range(max(0, per_group * group - 1), min(cells, per_group * group + per_group + 1))
+        for cell in range(low, high):
+            if cell not in written:
+                band_ref[:, pl.ds(cell * channels, channels), pl.ds(128 * group, 128)] = jnp.zeros(
+                    (band_ref.shape[0], channels, 128), band_ref.dtype
                 )
 
 
@@ -165,7 +178,7 @@
                 barrier, 1, device_id=(place[0] + one, place[1] + two),
                 device_id_type=pl.DeviceIdType.MESH,
             )
-    band_ref[...] = jnp.zeros(band_ref.shape, band_ref.dtype)
+    zero_band(band_ref, 32)
     fill_up(up_vmem, table_ref, up_ref, up_sems)
     count = sum(p.astype(jnp.int32) for p in present)
     pl.semaphore_wait(barrier, count)

time: 20.5 us -> 20.5 us (level)
  no operation moved by 1% of the time
where the time goes in v16:
time: 20.5 us; the launch traced here: 20.4 us
  Pallas kernels  18.7 us (91%)
  local copies, waits for them, and re-layouts  1.67 us (8%)
    pallas_call x1, Pallas kernels, body(): pl.pallas_call(lambda *refs: block_kernel(width, own_rows, own_cols, grid...  18.7 us
    unnamed x1, local copies, waits for them, and re-layouts  1.67 us

profile of v16, /device:TPU:193, one launch (start us, length us, event | category | flops | bytes accessed | tf_op | source)
XLA Modules:
  0.0 20.4 jit_solution(3958434020687787086)
XLA Ops:
  0.0 18.7 %shard_map.55 = bf16[16,16,512]{2,1,0:T(8,128)(2,1)} custom-call(bf16[4,4,128]{2,1,0:T(4,128)(2,1)} %refs_0_.1, bf16[16384,32]{1,0:T(8,128)(2,1)} %bitcast.3, bf16[480,640]{1,0:T(8,128)(2,1)} %constant.2.clone.refs_2_, bf16[864,32]{1,0:T(8,128)(2,1)} %bitcast.4, bf16[864,32]{1,0:T(8,128)(2,1)} %bitcast.5), custom_call_target="tpu_custom_call" | custom-call | tf_op jit(solution)/shard_map/pallas_call | solution.py:284
  18.7 1.7 %copy.7 = bf16[16,16,512]{2,1,0:T(8,128)(2,1)} copy(bf16[16,16,512]{2,1,0:T(8,128)(2,1)} %shard_map.55) | data formatting | bytes 524288

commit v17 on v14

--- a/solution.py
+++ b/solution.py
@@ -91,7 +91,11 @@
             weight_ref[pl.ds(start, chunk * span)], spread_out, preferred_element_type=jnp.float32
         )
         for part in range(chunk):
-            table_ref[step * chunk + part, pl.ds(3 * channels, channels), :] = jnp.zeros(
+            taps = step * chunk + part
+            one, two = taps // 8, taps % 8
+            phase = (one % 4) * 4 + two % 4
+            first_row = ((one // 4) * 2 + two // 4) * 4 * channels
+            table_ref[phase, pl.ds(pl.multiple_of(first_row + 3 * channels, channels), channels), :] = jnp.zeros(
                 (channels, 128), table_ref.dtype
             )
             for cell in range(3):
@@ -101,12 +105,12 @@
                     if 0 <= depth < 8:
                         row = part * span + depth * channels
                         block = jnp.where(quarter == out_cell, tiled[row : row + channels], block)
-                table_ref[step * chunk + part, pl.ds(cell * channels, channels), :] = block.astype(
+                table_ref[phase, pl.ds(pl.multiple_of(first_row + cell * channels, channels), channels), :] = block.astype(
                     table_ref.dtype
                 )
         return carry
 
-    lax.fori_loop(0, table_ref.shape[0] // chunk, one, 0)
+    lax.fori_loop(0, weight_ref.shape[0] // span // chunk, one, 0)
 
 
 DIRECTIONS = [(-1, -1), (-1, 0), (-1, 1), (0, -1), (0, 1), (1, -1), (1, 0), (1, 1)]
@@ -199,7 +203,7 @@
     span = 8
     ext = halo_rows(own_ref, staging_ref, size_one, span)
     groups = 4
-    channels = table_ref.shape[1] // groups
+    channels = table_ref.shape[1] // (4 * groups)
     lane = lax.broadcasted_iota(jnp.int32, ((size_one + 1) * span, 128), 1)
     windows = []
     for high_one in (0, 1):
@@ -220,18 +224,11 @@
                 parts.append(jnp.where(keep, rolled, 0.0))
             windows.append(jnp.concatenate(parts, axis=0).astype(jnp.bfloat16))
     rows_in = (size_one + 1) * span
+    stacked = jnp.concatenate(windows, axis=1)
     phases = []
     for phase_one in range(4):
         for phase_two in range(4):
-            total = None
-            for high_one in (0, 1):
-                for high_two in (0, 1):
-                    taps = (4 * high_one + phase_one) * 8 + 4 * high_two + phase_two
-                    term = jnp.dot(
-                        windows[high_one * 2 + high_two], table_ref[taps],
-                        preferred_element_type=jnp.float32,
-                    )
-                    total = term if total is None else total + term
+            total = jnp.dot(stacked, table_ref[phase_one * 4 + phase_two], preferred_element_type=jnp.float32)
             phases.append(
                 jnp.concatenate([total[g * rows_in : (g + 1) * rows_in] for g in range(groups)], axis=1)
             )
@@ -275,7 +272,7 @@
         out_specs=vmem,
         scratch_shapes=[
             pltpu.VMEM((9, lanes, lanes), jnp.bfloat16),
-            pltpu.VMEM((64, 4 * channels, 128), jnp.bfloat16),
+            pltpu.VMEM((16, 16 * channels, 128), jnp.bfloat16),
             pltpu.VMEM((len(DIRECTIONS),) + coarse_field.shape, coarse_field.dtype),
             pltpu.SemaphoreType.DMA((len(DIRECTIONS),)),
             pltpu.SemaphoreType.DMA((len(DIRECTIONS),)),

time: 20.5 us -> 21.1 us (1.029)
  Pallas kernels: 18.7 us -> 19.3 us
    pallas_call x1, Pallas kernels: 18.7 us -> 19.3 us  [body(): pl.pallas_call(lambda *refs: block_kernel(width, own_rows, own_cols, grid...]
where the time goes in v17:
time: 21.1 us; the launch traced here: 20.9 us
  Pallas kernels  19.3 us (91%)
  local copies, waits for them, and re-layouts  1.67 us (8%)
    pallas_call x1, Pallas kernels, body(): pl.pallas_call(lambda *refs: block_kernel(width, own_rows, own_cols, grid...  19.3 us
    unnamed x1, local copies, waits for them, and re-layouts  1.67 us

profile of v17, /device:TPU:193, one launch (start us, length us, event | category | flops | bytes accessed | tf_op | source)
XLA Modules:
  0.0 20.9 jit_solution(8458408088580628254)
XLA Ops:
  0.0 19.3 %shard_map.55 = bf16[16,16,512]{2,1,0:T(8,128)(2,1)} custom-call(bf16[4,4,128]{2,1,0:T(4,128)(2,1)} %refs_0_.1, bf16[16384,32]{1,0:T(8,128)(2,1)} %bitcast.3, bf16[480,640]{1,0:T(8,128)(2,1)} %constant.2.clone.refs_2_, bf16[864,32]{1,0:T(8,128)(2,1)} %bitcast.4, bf16[864,32]{1,0:T(8,128)(2,1)} %bitcast.5), custom_call_target="tpu_custom_call" | custom-call | tf_op jit(solution)/shard_map/pallas_call | solution.py:268
  19.3 1.7 %copy.7 = bf16[16,16,512]{2,1,0:T(8,128)(2,1)} copy(bf16[16,16,512]{2,1,0:T(8,128)(2,1)} %shard_map.55) | data formatting | bytes 524288

commit v18 on v14

--- a/solution.py
+++ b/solution.py
@@ -78,7 +78,7 @@
     per_group = 128 // channels
     span = 8 * channels
 
-    chunk = 16
+    chunk = 32
 
     def one(step, carry):
         start = pl.multiple_of(step * chunk * span, chunk * span)
@@ -280,7 +280,7 @@
             pltpu.SemaphoreType.DMA((len(DIRECTIONS),)),
             pltpu.SemaphoreType.DMA((len(DIRECTIONS),)),
             pltpu.VMEM((up_weight.size // channels, channels), up_weight.dtype),
-            pltpu.SemaphoreType.DMA((4,)),
+            pltpu.SemaphoreType.DMA((2,)),
         ],
         compiler_params=pltpu.CompilerParams(collective_id=0, has_side_effects=True),
     )(

time: 20.5 us -> 20.6 us (level)
  no operation moved by 1% of the time
where the time goes in v18:
time: 20.6 us; the launch traced here: 20.5 us
  Pallas kernels  18.8 us (91%)
  local copies, waits for them, and re-layouts  1.67 us (8%)
    pallas_call x1, Pallas kernels, body(): pl.pallas_call(lambda *refs: block_kernel(width, own_rows, own_cols, grid...  18.8 us
    unnamed x1, local copies, waits for them, and re-layouts  1.67 us

profile of v18, /device:TPU:193, one launch (start us, length us, event | category | flops | bytes accessed | tf_op | source)
XLA Modules:
  0.0 20.5 jit_solution(14782038444237874073)
XLA Ops:
  0.0 18.8 %shard_map.55 = bf16[16,16,512]{2,1,0:T(8,128)(2,1)} custom-call(bf16[4,4,128]{2,1,0:T(4,128)(2,1)} %refs_0_.1, bf16[16384,32]{1,0:T(8,128)(2,1)} %bitcast.3, bf16[480,640]{1,0:T(8,128)(2,1)} %constant.2.clone.refs_2_, bf16[864,32]{1,0:T(8,128)(2,1)} %bitcast.4, bf16[864,32]{1,0:T(8,128)(2,1)} %bitcast.5), custom_call_target="tpu_custom_call" | custom-call | tf_op jit(solution)/shard_map/pallas_call | solution.py:271
  18.8 1.7 %copy.7 = bf16[16,16,512]{2,1,0:T(8,128)(2,1)} copy(bf16[16,16,512]{2,1,0:T(8,128)(2,1)} %shard_map.55) | data formatting | bytes 524288
